TPU v7x, 1024 devices: a whole 8x8x8 slice. The times are simulated.
1024 devices in a mesh: dp: 8 (over y), expert: 64 (over x, z), mp: 2 (over core).
Axes of the slice: x: 8, y: 8, z: 8, core: 2. Of those that a mesh axis runs over, the one named last changes fastest.
Arguments:
- tokens: float32 [65536, 1024], P(('dp', 'expert')), may hold values from -24 to 24
- block_experts: int32 [16384, 1], P(('dp', 'expert')), may hold values from 0 to 63, as said below
- weight_up: bfloat16 [64, 1024, 2048], P('expert', None, 'mp'), may hold values from -0.1875 to 0.1875
- weight_down: bfloat16 [64, 2048, 1024], P('expert', 'mp'), may hold values from -0.125 to 0.125
- upstream: float32 [65536, 1024], P(('dp', 'expert')), may hold values from -24 to 24
Outputs:
- layer_output: float32 [65536, 1024], P(('dp', 'expert'))
- grad_tokens: float32 [65536, 1024], P(('dp', 'expert'))
- grad_up: float32 [64, 1024, 2048], P('expert', 'dp', 'mp')
- grad_down: float32 [64, 2048, 1024], P('expert', 'mp', 'dp')
Inputs may be any that keep to these rules, and one draw needn't show every extreme that they name: `block_experts`: of the 32 cell blocks of one device, at most 1 name the same expert, and in every draw some expert is named by exactly 1 block of every device.
All inputs are finite; a program needn't handle non-finite values.
Results may differ from a plain program's by a relative error of at most 0.015.
Values may be sent and summed in bfloat16 or wider, within the bound.
No kernel may reach another device: no remote copies, remote signals or barrier semaphores. Data moves between devices by JAX's collectives and lax.ppermute only.
A program may use at most 64 MiB of HBM per device.

v0:
```python
import jax
import jax.numpy as jnp
from jax import lax
from jax.sharding import PartitionSpec as P


def body(tokens, block_experts, weight_up, weight_down, upstream):
    experts = lax.axis_size("expert")
    blocks_dev = block_experts.shape[0]
    tok_rows = tokens.shape[0]
    width = tokens.shape[1]
    block = tok_rows // blocks_dev
    capacity = max(1, blocks_dev * 2 // experts)
    slot_total = experts * capacity
    labels = block_experts[:, 0]
    order = jnp.arange(blocks_dev, dtype=jnp.int32)
    earlier = order[None, :] < order[:, None]
    matches = labels[:, None] == labels[None, :]
    block_rank = jnp.sum(jnp.logical_and(matches, earlier).astype(jnp.int32), axis=1)
    slot_of_block = labels * capacity + block_rank
    slot_match = slot_of_block[None, :] == jnp.arange(slot_total, dtype=jnp.int32)[:, None]
    source_block = jnp.sum(jnp.where(slot_match, order[None, :], 0), axis=1)
    occupied = jnp.any(slot_match, axis=1)

    def dispatch(rows_lo):
        blocks = rows_lo.reshape(blocks_dev, block, width)
        picked = jnp.take(blocks, source_block, axis=0)
        filled = jnp.where(occupied[:, None, None], picked, jnp.zeros((), rows_lo.dtype))
        arrived = lax.all_to_all(filled, "expert", split_axis=0, concat_axis=0, tiled=True)
        return arrived.reshape(-1, width)

    def bring_home(partial_value):
        shaped = partial_value.reshape(experts, capacity * block, width)
        returned = lax.all_to_all(
            shaped.astype(jnp.bfloat16), "expert", split_axis=0, concat_axis=0, tiled=True
        ).astype(shaped.dtype)
        mine = jnp.take(returned, slot_of_block, axis=0)
        result = lax.psum(mine.reshape(tok_rows, width).astype(jnp.bfloat16), "mp").astype(
            jnp.float32
        )
        return result

    up_matrix = weight_up[0]
    down_matrix = weight_down[0]
    contract_last = (((1,), (1,)), ((), ()))
    contract_first = (((0,), (0,)), ((), ()))
    routed_lo = dispatch(tokens.astype(jnp.bfloat16))
    pre_act = jnp.dot(routed_lo, up_matrix, preferred_element_type=jnp.float32)
    hidden = jax.nn.gelu(pre_act).astype(jnp.bfloat16)
    mixed_part = jnp.dot(hidden, down_matrix, preferred_element_type=jnp.float32)
    layer_output = tokens + bring_home(mixed_part)
    routed_up = dispatch(upstream.astype(jnp.bfloat16))
    hidden_grad = lax.dot_general(
        routed_up, down_matrix, contract_last, preferred_element_type=jnp.float32
    )
    unused, gelu_back = jax.vjp(jax.nn.gelu, pre_act)
    pre_grad = gelu_back(hidden_grad)[0].astype(jnp.bfloat16)
    token_part = lax.dot_general(
        pre_grad, up_matrix, contract_last, preferred_element_type=jnp.float32
    )
    up_part = lax.dot_general(
        routed_lo, pre_grad, contract_first, preferred_element_type=jnp.float32
    )
    down_part = lax.dot_general(
        hidden, routed_up, contract_first, preferred_element_type=jnp.float32
    )
    grad_tokens = upstream + bring_home(token_part)
    grad_up, grad_down = (
        lax.psum_scatter(
            up_part[None].astype(jnp.bfloat16), "dp", scatter_dimension=1, tiled=True
        ).astype(jnp.float32),
        lax.psum_scatter(
            down_part[None].astype(jnp.bfloat16), "dp", scatter_dimension=2, tiled=True
        ).astype(jnp.float32),
    )
    return (layer_output, grad_tokens, grad_up, grad_down)


def solution(mesh):
    placed = (
        P(("dp", "expert"), None),
        P(("dp", "expert"), None),
        P("expert", None, "mp"),
        P("expert", "mp", None),
        P(("dp", "expert"), None),
    )
    return jax.shard_map(
        body,
        mesh=mesh,
        in_specs=placed,
        out_specs=(
            P(("dp", "expert"), None),
            P(("dp", "expert"), None),
            P("expert", "dp", "mp"),
            P("expert", "mp", "dp"),
        ),
        check_vma=False,
    )
```

profile of v0, /device:TPU:1, one launch (start us, length us, event | category | flops | bytes accessed | tf_op | source)
XLA Modules:
  0.0 262.4 jit_solution(15150161134508261944)
XLA Ops:
  9.9 1.1 convert_element_type.64
  11.1 1.1 convert_element_type.71
  13.3 1.8 gather_fusion.2
  15.0 2.5 select_select_fusion
  17.6 39.3 %all_to_all.20 = bf16[64,4,1024]{2,1,0:T(4,128)(2,1)S(1)} all-to-all(bf16[64,4,1024]{2,1,0:T(4,128)(2,1)S(1)} %get-tuple-element.11), channel_id=1, replica_groups=mesh['dp'=8,'expert'=64,'mp'=2] {'expert'}, dimensions={0} | all-to-all | bytes 1048576 | tf_op jit(solution)/shard_map/all_to_all | solution.py:29
  56.9 7.8 %all-to-all-start.2 = ((bf16[64,4,1024]{2,1,0:T(4,128)(2,1)}), bf16[64,4,1024]{2,1,0:T(4,128)(2,1)S(1)}, u32[]{:S(2)}, u32[]{:S(2)}) async-start(bf16[64,4,1024]{2,1,0:T(4,128)(2,1)} %get-tuple-element.10), calls=%async_computation.2 | async-start | bytes 1048576 | tf_op jit(solution)/shard_map/all_to_all | solution.py:29
  65.6 3.0 %multiply_convert_fusion = (bf16[256,1024]{1,0:T(8,128)(2,1)}, f32[256,1024]{1,0:T(8,128)}) fusion(bf16[256,1024]{1,0:T(8,128)(2,1)} %reshape.50, bf16[1,1024,1024]{2,1,0:T(8,128)(2,1)S(1)} %copy-done), kind=kOutput, calls=%fused_computation.26 | convolution fusion | flops 539230208 | bytes 4194304 | tf_op jit(solution)/shard_map/dot_general | solution.py:48
  68.6 12.2 %all-to-all-done.2 = bf16[64,4,1024]{2,1,0:T(4,128)(2,1)S(1)} async-done(((bf16[64,4,1024]{2,1,0:T(4,128)(2,1)}), bf16[64,4,1024]{2,1,0:T(4,128)(2,1)S(1)}, u32[]{:S(2)}, u32[]{:S(2)}) %all-to-all-start.2) | async-done | bytes 524320 | tf_op jit(solution)/shard_map/all_to_all | solution.py:29
  81.7 3.3 %fusion.20 = bf16[256,1024]{1,0:T(8,128)(2,1)S(1)} fusion(f32[256,1024]{1,0:T(8,128)} %get-tuple-element.15, bf16[256,1024]{1,0:T(8,128)(2,1)} %reshape.52, bf16[1,1024,1024]{2,1,0:T(8,128)(2,1)} %param.12), kind=kOutput, calls=%fused_computation.25 | convolution fusion | flops 542113792 | bytes 4194304 | tf_op jit(solution)/shard_map/dot_general | solution.py:53
  86.0 1.8 fusion.11
  87.8 1.2 copy.22
  89.0 7.5 %all-to-all-start.3 = ((bf16[64,4,1024]{2,1,0:T(4,128)(2,1)}), bf16[64,4,1024]{2,1,0:T(4,128)(2,1)S(1)}, u32[]{:S(2)}, u32[]{:S(2)}) async-start(bf16[64,4,1024]{2,1,0:T(4,128)(2,1)} %copy.22), calls=%async_computation.3 | async-start | bytes 1048576 | tf_op jit(solution)/shard_map/all_to_all | solution.py:34
  97.6 2.5 fusion.8
  100.1 1.2 copy.20
  101.3 11.0 %all-to-all-done.3 = bf16[64,4,1024]{2,1,0:T(4,128)(2,1)S(1)} async-done(((bf16[64,4,1024]{2,1,0:T(4,128)(2,1)}), bf16[64,4,1024]{2,1,0:T(4,128)(2,1)S(1)}, u32[]{:S(2)}, u32[]{:S(2)}) %all-to-all-start.3) | async-done | bytes 524320 | tf_op jit(solution)/shard_map/all_to_all | solution.py:34
  113.0 7.7 %all-to-all-start.1 = ((bf16[64,4,1024]{2,1,0:T(4,128)(2,1)}), bf16[64,4,1024]{2,1,0:T(4,128)(2,1)}, u32[]{:S(2)}, u32[]{:S(2)}) async-start(bf16[64,4,1024]{2,1,0:T(4,128)(2,1)} %copy.20), calls=%async_computation.1 | async-start | bytes 1048576 | tf_op jit(solution)/shard_map/all_to_all | solution.py:34
  120.9 1.8 gather_fusion.3
  122.8 12.9 %all-to-all-done.1 = bf16[64,4,1024]{2,1,0:T(4,128)(2,1)} async-done(((bf16[64,4,1024]{2,1,0:T(4,128)(2,1)}), bf16[64,4,1024]{2,1,0:T(4,128)(2,1)}, u32[]{:S(2)}, u32[]{:S(2)}) %all-to-all-start.1) | async-done | bytes 524320 | tf_op jit(solution)/shard_map/all_to_all | solution.py:34
  135.6 2.5 gather_fusion.1
  138.1 2.0 select_convert_fusion
  140.1 1.7 convert_element_type.76
  141.8 1.7 convert_element_type.69
  143.6 2.1 convert_bitcast_fusion
  145.7 10.9 %copy.23 = bf16[1,1024,1024]{1,0,2:T(2,128)(2,1)} copy(bf16[1,1024,1024]{2,1,0:T(8,128)(2,1)} %convert_bitcast_fusion) | data formatting | bytes 4194304
  156.6 4.3 %copy.31 = bf16[1024,1,1024]{2,0,1:T(8,128)(2,1)} copy(bf16[1024,1,1024]{2,1,0:T(2,128)(2,1)} %bitcast.39) | data formatting | bytes 4194304
  161.0 3.4 %convert_bitcast_fusion.1 = bf16[1,1024,1024]{2,1,0:T(8,128)(2,1)} fusion(bf16[256,1024]{1,0:T(8,128)(2,1)} %reshape.50, bf16[256,1024]{1,0:T(8,128)(2,1)} %copy-done.3), kind=kOutput, calls=%fused_computation.14 | convolution fusion | flops 537919488 | bytes 3145728 | tf_op jit(solution)/shard_map/dot_general | solution.py:61
  164.4 21.8 %all-reduce.3.cloned.1.call-done = (bf16[128,1024]{1,0:T(8,128)(2,1)}, bf16[128,1024]{1,0:T(8,128)(2,1)}) async-done(((bf16[128,1024]{1,0:T(8,128)(2,1)}, bf16[128,1024]{1,0:T(8,128)(2,1)}), (bf16[128,1024]{1,0:T(8,128)(2,1)}, bf16[128,1024]{1,0:T(8,128)(2,1)})) %all-reduce.3.cloned.1.call-update) | async-done | bytes 524304 | tf_op jit(solution)/shard_map/psum | solution.py:38
  186.2 2.1 convert_add_fusion
  188.3 14.5 %reduce-scatter.7.cloned.1.call-done = bf16[128,1024]{1,0:T(8,128)(2,1)} async-done(((bf16[1024,1024]{1,0:T(8,128)(2,1)}), bf16[128,1024]{1,0:T(8,128)(2,1)}) %reduce-scatter.7.cloned.1.call-update) | async-done | bytes 262160
  202.8 1.2 reshape_bitcast_fusion
  205.3 47.9 %reduce-scatter.5.cloned.1.call-done = bf16[1,128,1024]{2,1,0:T(8,128)(2,1)} async-done(((bf16[1,1024,1024]{2,1,0:T(8,128)(2,1)}), bf16[1,128,1024]{2,1,0:T(8,128)(2,1)}) %reduce-scatter.5.cloned.1.call-update) | async-done | bytes 262160 | tf_op jit(solution)/shard_map/reduce_scatter | solution.py:69
  253.2 1.8 convert_element_type.80
  (38 shorter events, 9.4 us)
Async XLA Ops:
  8.0 57.6 %copy-start = (bf16[1,1024,1024]{2,1,0:T(8,128)(2,1)S(1)}, bf16[1,1024,1024]{2,1,0:T(8,128)(2,1)}, u32[]{:S(2)}) copy-start(bf16[1,1024,1024]{2,1,0:T(8,128)(2,1)} %param.11) | copy-start | bytes 6291460
  56.9 23.9 %all-to-all-start.2 = ((bf16[64,4,1024]{2,1,0:T(4,128)(2,1)}), bf16[64,4,1024]{2,1,0:T(4,128)(2,1)S(1)}, u32[]{:S(2)}, u32[]{:S(2)}) async-start(bf16[64,4,1024]{2,1,0:T(4,128)(2,1)} %get-tuple-element.10), calls=%async_computation.2 | async-start | bytes 1048576 | tf_op jit(solution)/shard_map/all_to_all | solution.py:29
  85.0 2.9 %copy-start.3 = (bf16[256,1024]{1,0:T(8,128)(2,1)}, bf16[256,1024]{1,0:T(8,128)(2,1)S(1)}, u32[]{:S(2)}) copy-start(bf16[256,1024]{1,0:T(8,128)(2,1)S(1)} %fusion.20) | copy-start | bytes 1572868
  86.0 10.6 %copy-start.4 = (bf16[256,1024]{1,0:T(8,128)(2,1)S(1)}, bf16[256,1024]{1,0:T(8,128)(2,1)}, u32[]{:S(2)}) copy-start(bf16[256,1024]{1,0:T(8,128)(2,1)} %get-tuple-element.14) | copy-start | bytes 1572868
  89.0 23.2 %all-to-all-start.3 = ((bf16[64,4,1024]{2,1,0:T(4,128)(2,1)}), bf16[64,4,1024]{2,1,0:T(4,128)(2,1)S(1)}, u32[]{:S(2)}, u32[]{:S(2)}) async-start(bf16[64,4,1024]{2,1,0:T(4,128)(2,1)} %copy.22), calls=%async_computation.3 | async-start | bytes 1048576 | tf_op jit(solution)/shard_map/all_to_all | solution.py:34
  112.2 0.8 copy-start.6
  113.0 22.6 %all-to-all-start.1 = ((bf16[64,4,1024]{2,1,0:T(4,128)(2,1)}), bf16[64,4,1024]{2,1,0:T(4,128)(2,1)}, u32[]{:S(2)}, u32[]{:S(2)}) async-start(bf16[64,4,1024]{2,1,0:T(4,128)(2,1)} %copy.20), calls=%async_computation.1 | async-start | bytes 1048576 | tf_op jit(solution)/shard_map/all_to_all | solution.py:34
  120.7 23.0 %copy-start.5 = (bf16[256,1024]{1,0:T(8,128)(2,1)S(1)}, bf16[256,1024]{1,0:T(8,128)(2,1)}, u32[]{:S(2)}) copy-start(bf16[256,1024]{1,0:T(8,128)(2,1)} %reshape.52) | copy-start | bytes 1572868
  120.7 65.5 %all-reduce.3.cloned.1.call-start = ((), (), s32[]{:S(2)}) async-start(), calls=%async_computation.8 | async-start | bytes 1048576 | tf_op jit(solution)/shard_map/psum | solution.py:38
  143.6 59.2 %reduce-scatter.7.cloned.1.call-start = ((), (), s32[]{:S(2)}) async-start(), calls=%async_computation.7 | async-start | bytes 2359296
  160.9 25.3 %copy-start.1 = (f32[128,1024]{1,0:T(8,128)S(1)}, f32[128,1024]{1,0:T(8,128)}, u32[]{:S(2)}) copy-start(f32[128,1024]{1,0:T(8,128)} %param.13) | copy-start | bytes 1572868
  160.9 25.2 %copy-start.2 = (f32[128,1024]{1,0:T(8,128)S(1)}, f32[128,1024]{1,0:T(8,128)}, u32[]{:S(2)}) copy-start(f32[128,1024]{1,0:T(8,128)} %param.9) | copy-start | bytes 1572868
  161.0 92.2 %reduce-scatter.5.cloned.1.call-start = ((), (), s32[]{:S(2)}) async-start(), calls=%async_computation.6 | async-start | bytes 2359296 | tf_op jit(solution)/shard_map/reduce_scatter | solution.py:69
Sparse Core Ops, SparseCore 0:
  143.7 42.4 all-reduce.2
Sparse Core Ops, SparseCore 1:
  161.0 41.7 reduce-scatter.6
  206.5 46.7 reduce-scatter.4
where the time goes:
time: 267 us; the launch traced here: 262 us
  waiting for transfers between devices  120 us (45%)
  blocking collectives  39.3 us (15%)
  local copies, waits for them, and re-layouts  34.6 us (13%)
  starting transfers between devices  23.3 us (9%)
  matrix products  16.1 us (6%)
  between operations  15.7 us (6%)
  other arithmetic  13.3 us (5%)
    reduce_scatter x1, waiting for transfers between devices, body(): lax.psum_scatter(up_part[None].astype(jnp.bfloat16), 'dp', scatter_dimens...  47.9 us
    all_to_all x1, blocking collectives, dispatch(): lax.all_to_all(filled, 'expert', split_axis=0, concat_axis=0, tiled=True)  39.3 us
    all_to_all x2, waiting for transfers between devices, bring_home(): lax.all_to_all(shaped.astype(jnp.bfloat16), 'expert', split_axis=0, conca...  23.8 us
    psum x1, waiting for transfers between devices, bring_home(): lax.psum(mine.reshape(tok_rows, width).astype(jnp.bfloat16), 'mp')  21.8 us
    unnamed x18, local copies, waits for them, and re-layouts  17.7 us
    all_to_all x2, starting transfers between devices, bring_home(): lax.all_to_all(shaped.astype(jnp.bfloat16), 'expert', split_axis=0, conca...  15.2 us
    unnamed x4, waiting for transfers between devices  14.5 us
    all_to_all x1, waiting for transfers between devices, dispatch(): lax.all_to_all(filled, 'expert', split_axis=0, concat_axis=0, tiled=True)  12.2 us
  transfers between devices with their start and end apart: 6, of which 6 were waited for; matrix products, arithmetic and copies ran while one was open for 14% of the time, Pallas kernels for 0%

commit v1 on v0

v1 whole, which is shorter than its diff:
```python
import functools

import jax
import jax.numpy as jnp
from jax import lax
from jax.experimental import pallas as pl
from jax.experimental.pallas import tpu as pltpu
from jax.sharding import PartitionSpec as P

F32 = jnp.float32
BF16 = jnp.bfloat16
GELU_C = 0.7978845608028654
GELU_A = 0.044715
NN = (((1,), (0,)), ((), ()))
NT = (((1,), (1,)), ((), ()))
TN = (((0,), (0,)), ((), ()))


def iota(shape, axis):
    return lax.broadcasted_iota(jnp.int32, shape, axis)


def mm(a, b, dims):
    return lax.dot_general(a, b, dims, preferred_element_type=F32)


def label_column(labels):
    blocks = labels.shape[1]
    eye = iota((blocks, blocks), 0) == iota((blocks, blocks), 1)
    return jnp.sum(jnp.where(eye, labels, 0), axis=1, keepdims=True)


def slots_kernel(block, m_ref, labels_ref, tok_ref, up_ref, out_ref):
    rows = tok_ref.shape[0]
    blocks = labels_ref.shape[1]
    column = label_column(labels_ref[...])
    spread = iota((blocks, rows), 1) // block == iota((blocks, rows), 0)
    label_row = jnp.sum(jnp.where(spread, column, 0), axis=0, keepdims=True)
    dest = label_row * (2 * block) + iota((1, rows), 1) % block
    out_rows = iota((out_ref.shape[0], rows), 0)
    pick_tok = (out_rows == dest).astype(F32).astype(BF16)
    pick_up = (out_rows == dest + block).astype(F32).astype(BF16)
    total = mm(pick_tok, tok_ref[...].astype(BF16), NN)
    total = total + mm(pick_up, up_ref[...].astype(BF16), NN)
    out_ref[...] = total.astype(BF16)


def split_rows(rows, block):
    half = rows // 2
    i = iota((rows, rows), 0)
    j = lax.rem(i, half)
    source = (j // block) * (2 * block) + lax.rem(j, block) + jnp.where(i >= half, block, 0)
    return (iota((rows, rows), 1) == source).astype(F32).astype(BF16)


def merge_rows(rows, block):
    half = rows // 2
    i = iota((rows, rows), 1)
    j = lax.rem(i, half)
    source = (j // block) * (2 * block) + lax.rem(j, block) + jnp.where(i >= half, block, 0)
    return (iota((rows, rows), 0) == source).astype(F32).astype(BF16)


def grads_kernel(block, m_ref, mine_ref, other_ref, up_ref, down_ref, part_ref, hid_ref, pg_ref, x_ref):
    rows, half_cols = mine_ref.shape
    half = rows // 2
    step = pl.program_id(0)

    @pl.when(step == 0)
    def _():
        first = m_ref[0] == 0
        perm = split_rows(rows, block)
        mine = mm(perm, mine_ref[...], NN).astype(BF16)
        other = mm(perm, other_ref[...], NN).astype(BF16)
        x_ref[:, :half_cols] = jnp.where(first, mine, other)
        x_ref[:, half_cols:] = jnp.where(first, other, mine)
        pre = mm(x_ref[:half, :], up_ref[...], NN)
        hidden_grad = mm(x_ref[half:, :], down_ref[...], NT)
        square = pre * pre
        t = jnp.tanh(GELU_C * (pre + GELU_A * (square * pre)))
        cdf = 0.5 * (1.0 + t)
        slope = cdf + 0.5 * pre * (1.0 - t * t) * (GELU_C * (1.0 + 3.0 * GELU_A * square))
        hid_ref[...] = (pre * cdf).astype(BF16)
        pg_ref[...] = (hidden_grad * slope).astype(BF16)

    share = part_ref.shape[0] // 2
    cols = pl.ds(pl.multiple_of(step * share, share), share)
    part_ref[:share, :] = mm(x_ref[:half, cols], pg_ref[...], TN).astype(BF16)
    part_ref[share:, :] = mm(x_ref[half:, cols], hid_ref[...], TN).astype(BF16)


def returns_kernel(m_ref, hid_ref, pg_ref, up_ref, down_ref, keep_ref, send_ref):
    half = hid_ref.shape[0]
    half_cols = keep_ref.shape[1]
    first = m_ref[0] == 0
    mixed = mm(hid_ref[...], down_ref[...], NN)
    tgrad = mm(pg_ref[...], up_ref[...], NT)
    for k, value in ((0, mixed), (1, tgrad)):
        low, high = value[:, :half_cols], value[:, half_cols:]
        at = slice(k * half, (k + 1) * half)
        keep_ref[at, :] = jnp.where(first, low, high)
        send_ref[at, :] = jnp.where(first, high, low).astype(BF16)


def add_kernel(block, keep_ref, got_ref, out_ref):
    total = (keep_ref[...] + got_ref[...].astype(F32)).astype(BF16)
    out_ref[...] = mm(merge_rows(total.shape[0], block), total, NN).astype(BF16)


def home_kernel(block, labels_ref, back_ref, out_ref):
    rows = out_ref.shape[0] // 2
    blocks = labels_ref.shape[1]
    spread = iota((rows, blocks), 0) // block == iota((rows, blocks), 1)
    label = jnp.sum(jnp.where(spread, labels_ref[...], 0), axis=1, keepdims=True)
    dest = label * (2 * block) + iota((rows, 1), 0) % block
    columns = iota((rows, back_ref.shape[0]), 1)
    back = back_ref[...]
    for k in range(2):
        pick = (columns == dest + k * block).astype(F32).astype(BF16)
        out_ref[k * rows : (k + 1) * rows, :] = mm(pick, back, NN).astype(BF16)


def final_kernel(m_ref, mine_ref, other_ref, tok_ref, up_ref, out_ref, grad_ref):
    rows = tok_ref.shape[0]
    half_cols = mine_ref.shape[1]
    first = m_ref[0] == 0
    mine = mine_ref[...].astype(F32)
    other = other_ref[...].astype(F32)
    low = jnp.where(first, mine, other)
    high = jnp.where(first, other, mine)
    out_ref[:, :half_cols] = tok_ref[:, :half_cols] + low[:rows]
    out_ref[:, half_cols:] = tok_ref[:, half_cols:] + high[:rows]
    grad_ref[:, :half_cols] = up_ref[:, :half_cols] + low[rows:]
    grad_ref[:, half_cols:] = up_ref[:, half_cols:] + high[rows:]


def unpack_kernel(part_ref, up_ref, down_ref):
    share = up_ref.shape[0]
    up_ref[...] = part_ref[:share, :].astype(F32)
    down_ref[...] = part_ref[share:, :].astype(F32).T


def call(kernel, outs, scalars, name):
    one = not isinstance(outs, tuple)
    specs = [pl.BlockSpec(memory_space=pltpu.VMEM)]

    def run(*args):
        arrays = args[scalars:]
        return pl.pallas_call(
            kernel,
            out_shape=outs,
            in_specs=[pl.BlockSpec(memory_space=pltpu.SMEM)] * scalars + specs * len(arrays),
            out_specs=specs[0] if one else tuple(specs * len(outs)),
            name=name,
        )(*args)

    return run


def shape(dims, dtype):
    return jax.ShapeDtypeStruct(dims, dtype)


def body(tokens, block_experts, weight_up, weight_down, upstream):
    experts = lax.axis_size("expert")
    groups = lax.axis_size("dp")
    blocks_dev = block_experts.shape[0]
    tok_rows, width = tokens.shape
    block = tok_rows // blocks_dev
    half_cols = width // 2
    hidden_cols = weight_up.shape[2]
    slot_rows = experts * block
    rows = 2 * slot_rows
    share = width // groups
    m = lax.axis_index("mp").astype(jnp.int32).reshape(1)
    labels = block_experts.reshape(1, blocks_dev)
    swap = [(0, 1), (1, 0)]

    def exchange(value):
        shaped = value.reshape(experts, 2 * block, half_cols)
        moved = lax.all_to_all(shaped, "expert", split_axis=0, concat_axis=0, tiled=True)
        return moved.reshape(rows, half_cols)

    half_spec = pl.BlockSpec((tok_rows, half_cols), lambda i, m_ref: (0, m_ref[0]))
    slots = pl.pallas_call(
        functools.partial(slots_kernel, block),
        out_shape=shape((rows, half_cols), BF16),
        grid_spec=pltpu.PrefetchScalarGridSpec(
            num_scalar_prefetch=1,
            grid=(1,),
            in_specs=[pl.BlockSpec((1, blocks_dev), lambda i, m_ref: (0, 0)), half_spec, half_spec],
            out_specs=pl.BlockSpec((rows, half_cols), lambda i, m_ref: (0, 0)),
        ),
        name="slots",
    )(m, labels, tokens, upstream)
    mine = exchange(slots)
    other = lax.ppermute(mine, "mp", swap)

    up_matrix = weight_up[0]
    down_matrix = weight_down[0]

    def whole(array):
        return pl.BlockSpec(array.shape, lambda i, m_ref: (0, 0))

    half_shape = shape((slot_rows, hidden_cols), BF16)
    parts, hidden, pre_grad = pl.pallas_call(
        functools.partial(grads_kernel, block),
        out_shape=(shape((2 * width, hidden_cols), BF16), half_shape, half_shape),
        grid_spec=pltpu.PrefetchScalarGridSpec(
            num_scalar_prefetch=1,
            grid=(groups,),
            in_specs=[whole(mine), whole(other), whole(up_matrix), whole(down_matrix)],
            out_specs=(
                pl.BlockSpec((2 * share, hidden_cols), lambda i, m_ref: (i, 0)),
                whole(half_shape),
                whole(half_shape),
            ),
            scratch_shapes=[pltpu.VMEM((rows, width), BF16)],
        ),
        name="grads",
    )(m, mine, other, up_matrix, down_matrix)
    summed = lax.psum_scatter(parts, "dp", scatter_dimension=0, tiled=True)

    keep, send = call(
        returns_kernel, (shape((rows, half_cols), F32), shape((rows, half_cols), BF16)), 1, "returns"
    )(m, hidden, pre_grad, up_matrix, down_matrix)
    got = lax.ppermute(send, "mp", swap)
    added = call(functools.partial(add_kernel, block), shape((rows, half_cols), BF16), 0, "add")(keep, got)
    back = exchange(added)
    home = call(functools.partial(home_kernel, block), shape((2 * tok_rows, half_cols), BF16), 0, "home")(
        labels, back
    )
    home_other = lax.ppermute(home, "mp", swap)
    layer_output, grad_tokens = call(
        final_kernel, (shape(tokens.shape, F32), shape(tokens.shape, F32)), 1, "final"
    )(m, home, home_other, tokens, upstream)
    grad_up, grad_down = call(
        unpack_kernel, (shape((share, hidden_cols), F32), shape((hidden_cols, share), F32)), 0, "unpack"
    )(summed)
    return (layer_output, grad_tokens, grad_up[None], grad_down[None])


def solution(mesh):
    placed = (
        P(("dp", "expert"), None),
        P(("dp", "expert"), None),
        P("expert", None, "mp"),
        P("expert", "mp", None),
        P(("dp", "expert"), None),
    )
    return jax.shard_map(
        body,
        mesh=mesh,
        in_specs=placed,
        out_specs=(
            P(("dp", "expert"), None),
            P(("dp", "expert"), None),
            P("expert", "dp", "mp"),
            P("expert", "mp", "dp"),
        ),
        check_vma=False,
    )
```

time: 267 us -> 131 us (0.49); the launches traced: 262 us -> 130 us
  waiting for transfers between devices: 120 us -> 13 us
  local copies, waits for them, and re-layouts: 34.6 us -> 2.29 us
  Pallas kernels: 0 us -> 26.5 us
  blocking collectives: 39.3 us -> 62.3 us
  matrix products: 16.1 us -> 0 us
  other arithmetic: 13.3 us -> 0 us
  starting transfers between devices: 23.3 us -> 11.9 us
    reduce_scatter x1, waiting for transfers between devices: 47.9 us -> 8.43 us  [body(): summed = lax.psum_scatter(parts, 'dp', scatter_dimension=0, tiled=True)]
    all_to_all x3 -> x0, waiting for transfers between devices: 36 us -> none  [the longest x2 23.8 us: bring_home(): lax.all_to_all(shaped.astype(jnp.bfloat16), 'expert', split_axis=0, conca...]
    pallas_call x0 -> x7, Pallas kernels: none -> 26.5 us  [the longest x5 14.5 us: run(): pl.pallas_call(kernel, out_shape=outs, in_specs=[pl.BlockSpec(memory_spac...]
    all_to_all x1 -> x2, blocking collectives: 39.3 us -> 62.3 us  [exchange(): lax.all_to_all(shaped, 'expert', split_axis=0, concat_axis=0, tiled=True)]
    all_to_all x3 -> x0, starting transfers between devices: 23 us -> none  [the longest x2 15.2 us: bring_home(): lax.all_to_all(shaped.astype(jnp.bfloat16), 'expert', split_axis=0, conca...]
    psum x1 -> x0, waiting for transfers between devices: 21.8 us -> none  [bring_home(): lax.psum(mine.reshape(tok_rows, width).astype(jnp.bfloat16), 'mp')]
    dot_general x6 -> x0, matrix products: 16.1 us -> none  [the longest x1 3.35 us: body(): lax.dot_general(routed_lo, pre_grad, contract_first, preferred_element_ty...]
    unnamed x18 -> x8, local copies, waits for them, and re-layouts: 17.7 us -> 2.29 us
  transfers between devices with their start and end apart: 6 -> 4, of which waited for: 6 -> 4; matrix products, arithmetic and copies ran while one was open for 14% -> 0% of each run, Pallas kernels for 0% -> 10%
where the time goes in v1:
time: 131 us; the launch traced here: 130 us
  blocking collectives  62.3 us (48%)
  Pallas kernels  26.5 us (20%)
  between operations  14.1 us (11%)
  waiting for transfers between devices  13 us (10%)
  starting transfers between devices  11.9 us (9%)
  local copies, waits for them, and re-layouts  2.29 us (2%)
    all_to_all x2, blocking collectives, exchange(): lax.all_to_all(shaped, 'expert', split_axis=0, concat_axis=0, tiled=True)  62.3 us
    pallas_call x5, Pallas kernels, run(): pl.pallas_call(kernel, out_shape=outs, in_specs=[pl.BlockSpec(memory_spac...  14.5 us
    pallas_call x1, Pallas kernels, body(): pl.pallas_call(functools.partial(grads_kernel, block), out_shape=(shape((...  9.62 us
    reduce_scatter x1, waiting for transfers between devices, body(): summed = lax.psum_scatter(parts, 'dp', scatter_dimension=0, tiled=True)  8.43 us
    ppermute x1, starting transfers between devices, body(): other = lax.ppermute(mine, 'mp', swap)  5.78 us
    ppermute x1, starting transfers between devices, body(): home_other = lax.ppermute(home, 'mp', swap)  3.82 us
  transfers between devices with their start and end apart: 4, of which 4 were waited for; matrix products, arithmetic and copies ran while one was open for 0% of the time, Pallas kernels for 10%

profile of v1, /device:TPU:1, one launch (start us, length us, event | category | flops | bytes accessed | tf_op | source)
XLA Modules:
  0.0 130.1 jit_solution(16434507599446598992)
XLA Ops:
  7.2 0.0 reduce-scatter.2.cloned.1.call-start
  7.2 2.4 %slots.1 = bf16[512,512]{1,0:T(8,128)(2,1)} custom-call(s32[1]{0:T(128)} %bitcast.m_ref, s32[1,32]{1,0:T(1,128)} %bitcast.19, f32[128,1024]{1,0:T(8,128)} %tok_ref.3, f32[128,1024]{1,0:T(8,128)} %up_ref.3), custom_call_target="tpu_custom_call" | custom-call | tf_op jit(solution)/shard_map/slots/pallas_call | solution.py:185
  9.6 39.5 %all_to_all.10 = bf16[64,8,512]{2,1,0:T(8,128)(2,1)S(1)} all-to-all(bf16[64,8,512]{2,1,0:T(8,128)(2,1)} %bitcast.16), channel_id=1, replica_groups=mesh['dp'=8,'expert'=64,'mp'=2] {'expert'}, dimensions={0} | all-to-all | bytes 1048576 | tf_op jit(solution)/shard_map/all_to_all | solution.py:181
  49.1 0.0 copy-start
  49.1 5.8 %collective-permute-start = (bf16[512,512]{1,0:T(8,128)(2,1)S(1)}, bf16[512,512]{1,0:T(8,128)(2,1)S(1)}, u32[]{:S(2)}, u32[]{:S(2)}) collective-permute-start(bf16[512,512]{1,0:T(8,128)(2,1)S(1)} %bitcast.17), channel_id=1, source_target_pairs={{0,1},{1,0},{2,3},{3,2},{4,5},{5,4},{6,7},{7,6},{8,9},{9,8},{10,11... | collective-permute-start | bytes 1572872 | tf_op jit(solution)/shard_map/ppermute | solution.py:197
  54.9 1.5 %collective-permute-done.other_ref = bf16[512,512]{1,0:T(8,128)(2,1)S(1)} collective-permute-done((bf16[512,512]{1,0:T(8,128)(2,1)S(1)}, bf16[512,512]{1,0:T(8,128)(2,1)S(1)}, u32[]{:S(2)}, u32[]{:S(2)}) %collective-permute-start) | collective-permute-done | bytes 524320 | tf_op jit(solution)/shard_map/ppermute | solution.py:197
  56.4 0.0 copy-start.2
  56.4 0.0 copy-done
  56.4 0.8 copy-done.2
  57.2 9.6 %grads.1 = (bf16[2048,1024]{1,0:T(8,128)(2,1)}, bf16[256,1024]{1,0:T(8,128)(2,1)}, bf16[256,1024]{1,0:T(8,128)(2,1)}) custom-call(s32[1]{0:T(128)} %bitcast.m_ref, bf16[512,512]{1,0:T(8,128)(2,1)} %bitcast.18, bf16[512,512]{1,0:T(8,128)(2,1)} %copy-done.2, bf16[1024,1024]{1,0:T(8,128)(2,1)} %bitcast.10, bf16[1024,1024]{1,0:T(8,128)(2,1)} %bitcast.12), custom_call_target="tpu_custom_call" | custom-call | tf_op jit(solution)/shard_map/grads/pallas_call | solution.py:206
  66.8 0.0 reduce-scatter.2.cloned.1.call-update
  66.8 5.0 %returns.1 = (f32[512,512]{1,0:T(8,128)}, bf16[512,512]{1,0:T(8,128)(2,1)}) custom-call(s32[1]{0:T(128)} %bitcast.m_ref, bf16[256,1024]{1,0:T(8,128)(2,1)} %get-tuple-element.13.hid_ref, bf16[256,1024]{1,0:T(8,128)(2,1)} %get-tuple-element.14.pg_ref, bf16[1024,1024]{1,0:T(8,128)(2,1)} %bitcast.11, bf16[1024,1024]{1,0:T(8,128)(2,1)} %bitcast.13), custom_call_target="tpu_custom_call" | custom-call | tf_op jit(solution)/shard_map/returns/pallas_call | solution.py:149
  71.8 2.3 %collective-permute-start.1 = (bf16[512,512]{1,0:T(8,128)(2,1)}, bf16[512,512]{1,0:T(8,128)(2,1)S(1)}, u32[]{:S(2)}, u32[]{:S(2)}) collective-permute-start(bf16[512,512]{1,0:T(8,128)(2,1)} %get-tuple-element.16), channel_id=1, source_target_pairs={{0,1},{1,0},{2,3},{3,2},{4,5},{5,4},{6,7},{7,6},{8,9},{9,8},{10,11... | collective-permute-start | bytes 1572872 | tf_op jit(solution)/shard_map/ppermute | solution.py:227
  74.1 1.7 %collective-permute-done.1.got_ref = bf16[512,512]{1,0:T(8,128)(2,1)S(1)} collective-permute-done((bf16[512,512]{1,0:T(8,128)(2,1)}, bf16[512,512]{1,0:T(8,128)(2,1)S(1)}, u32[]{:S(2)}, u32[]{:S(2)}) %collective-permute-start.1) | collective-permute-done | bytes 524320 | tf_op jit(solution)/shard_map/ppermute | solution.py:227
  75.8 0.0 copy-start.1
  75.8 0.8 copy-done.1
  76.6 2.9 %add.4 = bf16[512,512]{1,0:T(8,128)(2,1)} custom-call(f32[512,512]{1,0:T(8,128)} %get-tuple-element.15.keep_ref, bf16[512,512]{1,0:T(8,128)(2,1)} %copy-done.1), custom_call_target="tpu_custom_call" | custom-call | tf_op jit(solution)/shard_map/add/pallas_call | solution.py:149
  79.4 22.8 %all_to_all.11 = bf16[64,8,512]{2,1,0:T(8,128)(2,1)} all-to-all(bf16[64,8,512]{2,1,0:T(8,128)(2,1)} %bitcast.15), channel_id=1, replica_groups=mesh['dp'=8,'expert'=64,'mp'=2] {'expert'}, dimensions={0} | all-to-all | bytes 1048576 | tf_op jit(solution)/shard_map/all_to_all | solution.py:181
  102.3 2.2 %home.1.mine_ref = bf16[256,512]{1,0:T(8,128)(2,1)} custom-call(s32[1,32]{1,0:T(1,128)} %bitcast.20, bf16[512,512]{1,0:T(8,128)(2,1)} %bitcast.14), custom_call_target="tpu_custom_call" | custom-call | tf_op jit(solution)/shard_map/home/pallas_call | solution.py:149
  104.4 3.8 %collective-permute-start.2 = (bf16[256,512]{1,0:T(8,128)(2,1)}, bf16[256,512]{1,0:T(8,128)(2,1)S(1)}, u32[]{:S(2)}, u32[]{:S(2)}) collective-permute-start(bf16[256,512]{1,0:T(8,128)(2,1)} %home.1.mine_ref), channel_id=1, source_target_pairs={{0,1},{1,0},{2,3},{3,2},{4,5},{5,4},{6,7},{7,6},{8,9},{9,8},{10,11... | collective-permute-start | bytes 786440 | tf_op jit(solution)/shard_map/ppermute | solution.py:233
  108.3 1.4 %collective-permute-done.2.other_ref = bf16[256,512]{1,0:T(8,128)(2,1)S(1)} collective-permute-done((bf16[256,512]{1,0:T(8,128)(2,1)}, bf16[256,512]{1,0:T(8,128)(2,1)S(1)}, u32[]{:S(2)}, u32[]{:S(2)}) %collective-permute-start.2) | collective-permute-done | bytes 262176 | tf_op jit(solution)/shard_map/ppermute | solution.py:233
  109.6 0.0 copy-start.3
  109.6 0.7 copy-done.3
  110.3 2.4 %final.1 = (f32[128,1024]{1,0:T(8,128)}, f32[128,1024]{1,0:T(8,128)}) custom-call(s32[1]{0:T(128)} %bitcast.m_ref, bf16[256,512]{1,0:T(8,128)(2,1)} %home.1.mine_ref, bf16[256,512]{1,0:T(8,128)(2,1)} %copy-done.3, f32[128,1024]{1,0:T(8,128)} %tok_ref.3, f32[128,1024]{1,0:T(8,128)} %up_ref.3), custom_call_target="tpu_custom_call" | custom-call | tf_op jit(solution)/shard_map/final/pallas_call | solution.py:149
  112.7 8.4 %reduce-scatter.2.cloned.1.call-done.part_ref = bf16[256,1024]{1,0:T(8,128)(2,1)} async-done(((bf16[2048,1024]{1,0:T(8,128)(2,1)}), bf16[256,1024]{1,0:T(8,128)(2,1)}) %reduce-scatter.2.cloned.1.call-update) | async-done | bytes 524304 | tf_op jit(solution)/shard_map/reduce_scatter | solution.py:222
  121.2 2.1 %unpack.1 = (f32[128,1024]{1,0:T(8,128)}, f32[1024,128]{1,0:T(8,128)}) custom-call(bf16[256,1024]{1,0:T(8,128)(2,1)} %reduce-scatter.2.cloned.1.call-done.part_ref), custom_call_target="tpu_custom_call" | custom-call | tf_op jit(solution)/shard_map/unpack/pallas_call | solution.py:149
Async XLA Ops:
  7.2 114.0 %reduce-scatter.2.cloned.1.call-start = ((), (), s32[]{:S(2)}) async-start(), calls=%async_computation.3 | async-start | bytes 4718592 | tf_op jit(solution)/shard_map/reduce_scatter | solution.py:222
  49.1 7.3 %copy-start = (bf16[64,8,512]{2,1,0:T(8,128)(2,1)}, bf16[64,8,512]{2,1,0:T(8,128)(2,1)S(1)}, u32[]{:S(2)}) copy-start(bf16[64,8,512]{2,1,0:T(8,128)(2,1)S(1)} %all_to_all.10) | copy-start | bytes 1572868
  49.1 7.3 %collective-permute-start = (bf16[512,512]{1,0:T(8,128)(2,1)S(1)}, bf16[512,512]{1,0:T(8,128)(2,1)S(1)}, u32[]{:S(2)}, u32[]{:S(2)}) collective-permute-start(bf16[512,512]{1,0:T(8,128)(2,1)S(1)} %bitcast.17), channel_id=1, source_target_pairs={{0,1},{1,0},{2,3},{3,2},{4,5},{5,4},{6,7},{7,6},{8,9},{9,8},{10,11... | collective-permute-start | bytes 1572872 | tf_op jit(solution)/shard_map/ppermute | solution.py:197
  56.4 0.8 copy-start.2
  71.8 4.0 %collective-permute-start.1 = (bf16[512,512]{1,0:T(8,128)(2,1)}, bf16[512,512]{1,0:T(8,128)(2,1)S(1)}, u32[]{:S(2)}, u32[]{:S(2)}) collective-permute-start(bf16[512,512]{1,0:T(8,128)(2,1)} %get-tuple-element.16), channel_id=1, source_target_pairs={{0,1},{1,0},{2,3},{3,2},{4,5},{5,4},{6,7},{7,6},{8,9},{9,8},{10,11... | collective-permute-start | bytes 1572872 | tf_op jit(solution)/shard_map/ppermute | solution.py:227
  75.8 0.8 copy-start.1
  104.4 5.2 %collective-permute-start.2 = (bf16[256,512]{1,0:T(8,128)(2,1)}, bf16[256,512]{1,0:T(8,128)(2,1)S(1)}, u32[]{:S(2)}, u32[]{:S(2)}) collective-permute-start(bf16[256,512]{1,0:T(8,128)(2,1)} %home.1.mine_ref), channel_id=1, source_target_pairs={{0,1},{1,0},{2,3},{3,2},{4,5},{5,4},{6,7},{7,6},{8,9},{9,8},{10,11... | collective-permute-start | bytes 786440 | tf_op jit(solution)/shard_map/ppermute | solution.py:233
  109.6 0.7 copy-start.3
Sparse Core Ops, SparseCore 0:
  66.9 54.1 reduce-scatter.1

commit v2 on v1

--- a/solution.py
+++ b/solution.py
@@ -61,17 +61,31 @@
     return (iota((rows, rows), 0) == source).astype(F32).astype(BF16)
 
 
-def grads_kernel(block, m_ref, mine_ref, other_ref, up_ref, down_ref, part_ref, hid_ref, pg_ref, x_ref):
+def front_kernel(block, mine_ref, up_ref, down_ref, x_ref, up_out, down_out, sems):
+    copies = [
+        pltpu.make_async_copy(up_ref, up_out, sems.at[0]),
+        pltpu.make_async_copy(down_ref, down_out, sems.at[1]),
+    ]
+    for copy in copies:
+        copy.start()
+    x_ref[...] = mm(split_rows(mine_ref.shape[0], block), mine_ref[...], NN).astype(BF16)
+    for copy in copies:
+        copy.wait()
+
+
+def grads_kernel(
+    block, share, m_ref, mine_ref, other_ref, up_ref, down_ref, part_ref, hid_ref, pg_ref, x_ref, hidt_ref
+):
     rows, half_cols = mine_ref.shape
     half = rows // 2
+    hidden_cols = hid_ref.shape[1]
     step = pl.program_id(0)
 
     @pl.when(step == 0)
     def _():
         first = m_ref[0] == 0
-        perm = split_rows(rows, block)
-        mine = mm(perm, mine_ref[...], NN).astype(BF16)
-        other = mm(perm, other_ref[...], NN).astype(BF16)
+        mine = mine_ref[...]
+        other = mm(split_rows(rows, block), other_ref[...], NN).astype(BF16)
         x_ref[:, :half_cols] = jnp.where(first, mine, other)
         x_ref[:, half_cols:] = jnp.where(first, other, mine)
         pre = mm(x_ref[:half, :], up_ref[...], NN)
@@ -80,13 +94,23 @@
         t = jnp.tanh(GELU_C * (pre + GELU_A * (square * pre)))
         cdf = 0.5 * (1.0 + t)
         slope = cdf + 0.5 * pre * (1.0 - t * t) * (GELU_C * (1.0 + 3.0 * GELU_A * square))
-        hid_ref[...] = (pre * cdf).astype(BF16)
+        hidden = (pre * cdf).astype(BF16)
+        hid_ref[...] = hidden
+        hidt_ref[...] = hidden.T
         pg_ref[...] = (hidden_grad * slope).astype(BF16)
 
-    share = part_ref.shape[0] // 2
-    cols = pl.ds(pl.multiple_of(step * share, share), share)
-    part_ref[:share, :] = mm(x_ref[:half, cols], pg_ref[...], TN).astype(BF16)
-    part_ref[share:, :] = mm(x_ref[half:, cols], hid_ref[...], TN).astype(BF16)
+    shares = part_ref.shape[0] // (2 * hidden_cols)
+    span = shares * share
+    cols = pl.ds(pl.multiple_of(step * span, span), span)
+    up_part = mm(x_ref[:half, cols], pg_ref[...], TN).astype(BF16)
+    down_part = mm(hidt_ref[...], x_ref[half:, cols], NN).astype(BF16)
+    for k in range(shares):
+        own = slice(k * share, (k + 1) * share)
+        base = 2 * k * hidden_cols
+        for j in range(hidden_cols // share):
+            at = slice(j * share, (j + 1) * share)
+            part_ref[base + j * share : base + (j + 1) * share, :] = up_part[own, at]
+        part_ref[base + hidden_cols : base + 2 * hidden_cols, :] = down_part[:, own]
 
 
 def returns_kernel(m_ref, hid_ref, pg_ref, up_ref, down_ref, keep_ref, send_ref):
@@ -135,22 +159,36 @@
 
 
 def unpack_kernel(part_ref, up_ref, down_ref):
-    share = up_ref.shape[0]
-    up_ref[...] = part_ref[:share, :].astype(F32)
-    down_ref[...] = part_ref[share:, :].astype(F32).T
+    hidden_cols, share = down_ref.shape
+    for j in range(hidden_cols // share):
+        at = slice(j * share, (j + 1) * share)
+        up_ref[:, at] = part_ref[at, :].astype(F32)
+    down_ref[...] = part_ref[hidden_cols:, :].astype(F32)
+
+
+PARAMS = pltpu.CompilerParams(vmem_limit_bytes=20 * 2**20)
+ONCHIP = pl.BlockSpec(memory_space=pltpu.VMEM)
+
+
+def onchip(array):
+    return pltpu.with_memory_space_constraint(array, pltpu.VMEM)
+
+
+def offchip(array):
+    return pltpu.with_memory_space_constraint(array, pltpu.HBM)
 
 
 def call(kernel, outs, scalars, name):
     one = not isinstance(outs, tuple)
-    specs = [pl.BlockSpec(memory_space=pltpu.VMEM)]
 
     def run(*args):
-        arrays = args[scalars:]
+        arrays = len(args) - scalars
         return pl.pallas_call(
             kernel,
             out_shape=outs,
-            in_specs=[pl.BlockSpec(memory_space=pltpu.SMEM)] * scalars + specs * len(arrays),
-            out_specs=specs[0] if one else tuple(specs * len(outs)),
+            in_specs=[pl.BlockSpec(memory_space=pltpu.SMEM)] * scalars + [ONCHIP] * arrays,
+            out_specs=ONCHIP if one else (ONCHIP,) * len(outs),
+            compiler_params=PARAMS,
             name=name,
         )(*args)
 
@@ -159,6 +197,65 @@
 
 def shape(dims, dtype):
     return jax.ShapeDtypeStruct(dims, dtype)
+
+
+def slots_call(block, rows, m, labels, tokens, upstream):
+    tok_rows, width = tokens.shape
+    half_spec = pl.BlockSpec((tok_rows, width // 2), lambda i, m_ref: (0, m_ref[0]))
+    return pl.pallas_call(
+        functools.partial(slots_kernel, block),
+        out_shape=pltpu.VMEM((rows, width // 2), BF16),
+        grid_spec=pltpu.PrefetchScalarGridSpec(
+            num_scalar_prefetch=1,
+            grid=(1,),
+            in_specs=[pl.BlockSpec(labels.shape, lambda i, m_ref: (0, 0)), half_spec, half_spec],
+            out_specs=ONCHIP,
+        ),
+        compiler_params=PARAMS,
+        name="slots",
+    )(m, offchip(labels), offchip(tokens), offchip(upstream))
+
+
+def front_call(block, mine, up_matrix, down_matrix):
+    anywhere = pl.BlockSpec(memory_space=pl.ANY)
+    return pl.pallas_call(
+        functools.partial(front_kernel, block),
+        out_shape=(
+            pltpu.VMEM(mine.shape, BF16),
+            pltpu.VMEM(up_matrix.shape, BF16),
+            pltpu.VMEM(down_matrix.shape, BF16),
+        ),
+        in_specs=[ONCHIP, anywhere, anywhere],
+        out_specs=(ONCHIP, ONCHIP, ONCHIP),
+        scratch_shapes=[pltpu.SemaphoreType.DMA((2,))],
+        compiler_params=PARAMS,
+        name="front",
+    )(onchip(mine), offchip(up_matrix), offchip(down_matrix))
+
+
+def grads_call(block, groups, m, mine, other, up_matrix, down_matrix):
+    rows = mine.shape[0]
+    width, hidden_cols = up_matrix.shape
+    share = width // groups
+    steps = max(1, groups // 4)
+    half_shape = pltpu.VMEM((rows // 2, hidden_cols), BF16)
+    return pl.pallas_call(
+        functools.partial(grads_kernel, block, share),
+        out_shape=(pltpu.HBM((2 * hidden_cols * groups, share), BF16), half_shape, half_shape),
+        grid_spec=pltpu.PrefetchScalarGridSpec(
+            num_scalar_prefetch=1,
+            grid=(steps,),
+            in_specs=[ONCHIP] * 4,
+            out_specs=(
+                pl.BlockSpec((2 * hidden_cols * groups // steps, share), lambda i, m_ref: (i, 0)),
+                ONCHIP,
+                ONCHIP,
+            ),
+            scratch_shapes=[pltpu.VMEM((rows, width), BF16), pltpu.VMEM((hidden_cols, rows // 2), BF16)],
+        ),
+        compiler_params=PARAMS,
+        name="grads",
+    )(m, onchip(mine), onchip(other), onchip(up_matrix), onchip(down_matrix))
 
 
 def body(tokens, block_experts, weight_up, weight_down, upstream):
@@ -169,8 +266,7 @@
     block = tok_rows // blocks_dev
     half_cols = width // 2
     hidden_cols = weight_up.shape[2]
-    slot_rows = experts * block
-    rows = 2 * slot_rows
+    rows = 2 * experts * block
     share = width // groups
     m = lax.axis_index("mp").astype(jnp.int32).reshape(1)
     labels = block_experts.reshape(1, blocks_dev)
@@ -181,62 +277,31 @@
         moved = lax.all_to_all(shaped, "expert", split_axis=0, concat_axis=0, tiled=True)
         return moved.reshape(rows, half_cols)
 
-    half_spec = pl.BlockSpec((tok_rows, half_cols), lambda i, m_ref: (0, m_ref[0]))
-    slots = pl.pallas_call(
-        functools.partial(slots_kernel, block),
-        out_shape=shape((rows, half_cols), BF16),
-        grid_spec=pltpu.PrefetchScalarGridSpec(
-            num_scalar_prefetch=1,
-            grid=(1,),
-            in_specs=[pl.BlockSpec((1, blocks_dev), lambda i, m_ref: (0, 0)), half_spec, half_spec],
-            out_specs=pl.BlockSpec((rows, half_cols), lambda i, m_ref: (0, 0)),
-        ),
-        name="slots",
-    )(m, labels, tokens, upstream)
-    mine = exchange(slots)
-    other = lax.ppermute(mine, "mp", swap)
-
-    up_matrix = weight_up[0]
-    down_matrix = weight_down[0]
-
-    def whole(array):
-        return pl.BlockSpec(array.shape, lambda i, m_ref: (0, 0))
-
-    half_shape = shape((slot_rows, hidden_cols), BF16)
-    parts, hidden, pre_grad = pl.pallas_call(
-        functools.partial(grads_kernel, block),
-        out_shape=(shape((2 * width, hidden_cols), BF16), half_shape, half_shape),
-        grid_spec=pltpu.PrefetchScalarGridSpec(
-            num_scalar_prefetch=1,
-            grid=(groups,),
-            in_specs=[whole(mine), whole(other), whole(up_matrix), whole(down_matrix)],
-            out_specs=(
-                pl.BlockSpec((2 * share, hidden_cols), lambda i, m_ref: (i, 0)),
-                whole(half_shape),
-                whole(half_shape),
-            ),
-            scratch_shapes=[pltpu.VMEM((rows, width), BF16)],
-        ),
-        name="grads",
-    )(m, mine, other, up_matrix, down_matrix)
+    slots = slots_call(block, rows, m, labels, tokens, upstream)
+    arrived = exchange(slots)
+    other = lax.ppermute(arrived, "mp", swap)
+    mine, up_matrix, down_matrix = front_call(block, arrived, weight_up[0], weight_down[0])
+    parts, hidden, pre_grad = grads_call(block, groups, m, mine, other, up_matrix, down_matrix)
     summed = lax.psum_scatter(parts, "dp", scatter_dimension=0, tiled=True)
 
     keep, send = call(
-        returns_kernel, (shape((rows, half_cols), F32), shape((rows, half_cols), BF16)), 1, "returns"
-    )(m, hidden, pre_grad, up_matrix, down_matrix)
+        returns_kernel, (pltpu.VMEM((rows, half_cols), F32), pltpu.VMEM((rows, half_cols), BF16)), 1, "returns"
+    )(m, onchip(hidden), onchip(pre_grad), weight_up[0], weight_down[0])
     got = lax.ppermute(send, "mp", swap)
-    added = call(functools.partial(add_kernel, block), shape((rows, half_cols), BF16), 0, "add")(keep, got)
+    added = call(functools.partial(add_kernel, block), pltpu.VMEM((rows, half_cols), BF16), 0, "add")(
+        onchip(keep), onchip(got)
+    )
     back = exchange(added)
-    home = call(functools.partial(home_kernel, block), shape((2 * tok_rows, half_cols), BF16), 0, "home")(
-        labels, back
+    home = call(functools.partial(home_kernel, block), pltpu.VMEM((2 * tok_rows, half_cols), BF16), 0, "home")(
+        labels, onchip(back)
     )
     home_other = lax.ppermute(home, "mp", swap)
     layer_output, grad_tokens = call(
         final_kernel, (shape(tokens.shape, F32), shape(tokens.shape, F32)), 1, "final"
-    )(m, home, home_other, tokens, upstream)
+    )(m, onchip(home), onchip(home_other), tokens, upstream)
     grad_up, grad_down = call(
         unpack_kernel, (shape((share, hidden_cols), F32), shape((hidden_cols, share), F32)), 0, "unpack"
-    )(summed)
+    )(offchip(summed))
     return (layer_output, grad_tokens, grad_up[None], grad_down[None])
 
 

time: 131 us -> 124 us (0.947)
  Pallas kernels: 26.5 us -> 13.7 us
  waiting for transfers between devices: 13 us -> 19.1 us
    pallas_call x5, Pallas kernels: 14.5 us -> 5.24 us  [run(): pl.pallas_call(kernel, out_shape=outs, in_specs=[pl.BlockSpec(memory_spac...]
    reduce_scatter x1, waiting for transfers between devices: 8.43 us -> 16 us  [body(): summed = lax.psum_scatter(parts, 'dp', scatter_dimension=0, tiled=True)]
    pallas_call x2 -> x3, Pallas kernels: 12 us -> 8.5 us  [the longest x1 4.68 us: grads_call(): pl.pallas_call(functools.partial(grads_kernel, block, share), out_shape=(...]
    ppermute x1, waiting for transfers between devices: 1.51 us -> 0.01 us  [body(): other = lax.ppermute(arrived, 'mp', swap)]
    unnamed x8 -> x10, local copies, waits for them, and re-layouts: 2.29 us -> 3.18 us
  transfers between devices with their start and end apart: 4 -> 4, of which waited for: 4 -> 3; matrix products, arithmetic and copies ran while one was open for 0% -> 0% of each run, Pallas kernels for 10% -> 4%
where the time goes in v2:
time: 124 us
  blocking collectives  61.5 us (50%)
  waiting for transfers between devices  19.1 us (15%)
  between operations  14.1 us (11%)
  Pallas kernels  13.7 us (11%)
  starting transfers between devices  12.3 us (10%)
  local copies, waits for them, and re-layouts  3.18 us (3%)
    all_to_all x2, blocking collectives, exchange(): lax.all_to_all(shaped, 'expert', split_axis=0, concat_axis=0, tiled=True)  61.5 us
    reduce_scatter x1, waiting for transfers between devices, body(): summed = lax.psum_scatter(parts, 'dp', scatter_dimension=0, tiled=True)  16 us
    ppermute x1, starting transfers between devices, body(): other = lax.ppermute(arrived, 'mp', swap)  5.78 us
    pallas_call x5, Pallas kernels, run(): pl.pallas_call(kernel, out_shape=outs, in_specs=[pl.BlockSpec(memory_spac...  5.24 us
    pallas_call x1, Pallas kernels, grads_call(): pl.pallas_call(functools.partial(grads_kernel, block, share), out_shape=(...  4.68 us
    ppermute x1, starting transfers between devices, body(): home_other = lax.ppermute(home, 'mp', swap)  4.45 us
    unnamed x10, local copies, waits for them, and re-layouts  3.18 us
  transfers between devices with their start and end apart: 4, of which 3 were waited for; matrix products, arithmetic and copies ran while one was open for 0% of the time, Pallas kernels for 4%

profile of v2, /device:TPU:1, one launch (start us, length us, event | category | flops | bytes accessed | tf_op | source)
XLA Modules:
  0.0 123.9 jit_solution(445924324583606599)
XLA Ops:
  7.2 0.0 reduce-scatter.2.cloned.1.call-start
  7.2 1.6 %slots.1 = bf16[512,512]{1,0:T(8,128)(2,1)S(1)} custom-call(s32[1]{0:T(128)} %bitcast.m_ref, s32[1,32]{1,0:T(1,128)} %bitcast.19, f32[128,1024]{1,0:T(8,128)} %tok_ref.3, f32[128,1024]{1,0:T(8,128)} %up_ref.3), custom_call_target="tpu_custom_call" | custom-call | tf_op jit(solution)/shard_map/slots/pallas_call | solution.py:205
  8.8 39.3 %all_to_all.10 = bf16[64,8,512]{2,1,0:T(8,128)(2,1)S(1)} all-to-all(bf16[64,8,512]{2,1,0:T(8,128)(2,1)S(1)} %bitcast.18), channel_id=1, replica_groups=mesh['dp'=8,'expert'=64,'mp'=2] {'expert'}, dimensions={0} | all-to-all | bytes 1048576 | tf_op jit(solution)/shard_map/all_to_all | solution.py:277
  48.1 5.8 %collective-permute-start = (bf16[512,512]{1,0:T(8,128)(2,1)S(1)}, bf16[512,512]{1,0:T(8,128)(2,1)S(1)}, u32[]{:S(2)}, u32[]{:S(2)}) collective-permute-start(bf16[512,512]{1,0:T(8,128)(2,1)S(1)} %bitcast.14), channel_id=1, source_target_pairs={{0,1},{1,0},{2,3},{3,2},{4,5},{5,4},{6,7},{7,6},{8,9},{9,8},{10,11... | collective-permute-start | bytes 1572872 | tf_op jit(solution)/shard_map/ppermute | solution.py:282
  53.9 2.3 %front.1 = (bf16[512,512]{1,0:T(8,128)(2,1)S(1)}, bf16[1024,1024]{1,0:T(8,128)(2,1)S(1)}, bf16[1024,1024]{1,0:T(8,128)(2,1)S(1)}) custom-call(bf16[512,512]{1,0:T(8,128)(2,1)S(1)} %bitcast.15, bf16[1024,1024]{1,0:T(8,128)(2,1)} %bitcast.10, bf16[1024,1024]{1,0:T(8,128)(2,1)} %bitcast.12), custom_call_target="tpu_custom_call" | custom-call | tf_op jit(solution)/shard_map/front/pallas_call | solution.py:221
  56.1 0.0 collective-permute-done.other_ref
  56.2 4.7 %grads.1 = (bf16[16384,128]{1,0:T(8,128)(2,1)}, bf16[256,1024]{1,0:T(8,128)(2,1)S(1)}, bf16[256,1024]{1,0:T(8,128)(2,1)S(1)}) custom-call(s32[1]{0:T(128)} %bitcast.m_ref, bf16[512,512]{1,0:T(8,128)(2,1)S(1)} %get-tuple-element.16.mine_ref, bf16[512,512]{1,0:T(8,128)(2,1)S(1)} %collective-permute-done.other_ref, ...), custom_call_target="tpu_custom_call" | custom-call | tf_op jit(solution)/shard_map/grads/pallas_call | solution.py:242
  60.8 0.0 copy-start
  60.8 0.0 reduce-scatter.2.cloned.1.call-update
  60.9 1.6 %copy-done = bf16[1,1024,1024]{2,1,0:T(8,128)(2,1)S(1)} copy-done((bf16[1,1024,1024]{2,1,0:T(8,128)(2,1)S(1)}, bf16[1,1024,1024]{2,1,0:T(8,128)(2,1)}, u32[]{:S(2)}) %copy-start) | copy-done | bytes 2097176
  62.4 0.0 copy-start.1
  62.4 1.6 %copy-done.1 = bf16[1,1024,1024]{2,1,0:T(8,128)(2,1)S(1)} copy-done((bf16[1,1024,1024]{2,1,0:T(8,128)(2,1)S(1)}, bf16[1,1024,1024]{2,1,0:T(8,128)(2,1)}, u32[]{:S(2)}) %copy-start.1) | copy-done | bytes 2097176
  64.0 1.3 %returns.1 = (f32[512,512]{1,0:T(8,128)S(1)}, bf16[512,512]{1,0:T(8,128)(2,1)S(1)}) custom-call(s32[1]{0:T(128)} %bitcast.m_ref, bf16[256,1024]{1,0:T(8,128)(2,1)S(1)} %get-tuple-element.19.hid_ref, bf16[256,1024]{1,0:T(8,128)(2,1)S(1)} %get-tuple-element.20.pg_ref, bf16[1024,1024]{1,0:T(8,128)(2,1)S(1)} %bitcast.11, bf16[1024,1024]{1,0:T(8,128)(2,1)S(1)} %bitcast.13), custom_call_target="tpu_custom_call" | custom-call | tf_op jit(solution)/shard_map/returns/pallas_call | solution.py:186
  65.3 0.0 copy-start.4
  65.3 0.0 copy-start.2
  65.3 0.0 copy-start.3
  65.3 2.1 %collective-permute-start.1 = (bf16[512,512]{1,0:T(8,128)(2,1)S(1)}, bf16[512,512]{1,0:T(8,128)(2,1)S(1)}, u32[]{:S(2)}, u32[]{:S(2)}) collective-permute-start(bf16[512,512]{1,0:T(8,128)(2,1)S(1)} %get-tuple-element.22), channel_id=1, source_target_pairs={{0,1},{1,0},{2,3},{3,2},{4,5},{5,4},{6,7},{7,6},{8,9},{9,8},{10,11... | collective-permute-start | bytes 1572872 | tf_op jit(solution)/shard_map/ppermute | solution.py:290
  67.4 1.9 %collective-permute-done.1.got_ref = bf16[512,512]{1,0:T(8,128)(2,1)S(1)} collective-permute-done((bf16[512,512]{1,0:T(8,128)(2,1)S(1)}, bf16[512,512]{1,0:T(8,128)(2,1)S(1)}, u32[]{:S(2)}, u32[]{:S(2)}) %collective-permute-start.1) | collective-permute-done | bytes 524320 | tf_op jit(solution)/shard_map/ppermute | solution.py:290
  69.3 0.5 add.4
  69.8 22.2 %all_to_all.11 = bf16[64,8,512]{2,1,0:T(8,128)(2,1)S(1)} all-to-all(bf16[64,8,512]{2,1,0:T(8,128)(2,1)S(1)} %bitcast.17), channel_id=1, replica_groups=mesh['dp'=8,'expert'=64,'mp'=2] {'expert'}, dimensions={0} | all-to-all | bytes 1048576 | tf_op jit(solution)/shard_map/all_to_all | solution.py:277
  91.9 0.0 copy-done.4
  91.9 0.4 home.1.mine_ref
  92.3 4.4 %collective-permute-start.2 = (bf16[256,512]{1,0:T(8,128)(2,1)S(1)}, bf16[256,512]{1,0:T(8,128)(2,1)S(1)}, u32[]{:S(2)}, u32[]{:S(2)}) collective-permute-start(bf16[256,512]{1,0:T(8,128)(2,1)S(1)} %home.1.mine_ref), channel_id=1, source_target_pairs={{0,1},{1,0},{2,3},{3,2},{4,5},{5,4},{6,7},{7,6},{8,9},{9,8},{10,11... | collective-permute-start | bytes 786440 | tf_op jit(solution)/shard_map/ppermute | solution.py:298
  96.8 1.1 collective-permute-done.2.other_ref
  97.9 0.0 copy-done.2
  97.9 0.0 copy-done.3
  97.9 1.0 final.1
  99.0 16.0 %reduce-scatter.2.cloned.1.call-done.part_ref = bf16[2048,128]{1,0:T(8,128)(2,1)} async-done(((bf16[16384,128]{1,0:T(8,128)(2,1)}), bf16[2048,128]{1,0:T(8,128)(2,1)}) %reduce-scatter.2.cloned.1.call-update) | async-done | bytes 524304 | tf_op jit(solution)/shard_map/reduce_scatter | solution.py:285
  115.0 2.1 %unpack.1 = (f32[128,1024]{1,0:T(8,128)}, f32[1024,128]{1,0:T(8,128)}) custom-call(bf16[2048,128]{1,0:T(8,128)(2,1)} %reduce-scatter.2.cloned.1.call-done.part_ref), custom_call_target="tpu_custom_call" | custom-call | tf_op jit(solution)/shard_map/unpack/pallas_call | solution.py:186
Async XLA Ops:
  7.2 107.8 %reduce-scatter.2.cloned.1.call-start = ((), (), s32[]{:S(2)}) async-start(), calls=%async_computation.3 | async-start | bytes 4718592 | tf_op jit(solution)/shard_map/reduce_scatter | solution.py:285
  48.1 8.1 %collective-permute-start = (bf16[512,512]{1,0:T(8,128)(2,1)S(1)}, bf16[512,512]{1,0:T(8,128)(2,1)S(1)}, u32[]{:S(2)}, u32[]{:S(2)}) collective-permute-start(bf16[512,512]{1,0:T(8,128)(2,1)S(1)} %bitcast.14), channel_id=1, source_target_pairs={{0,1},{1,0},{2,3},{3,2},{4,5},{5,4},{6,7},{7,6},{8,9},{9,8},{10,11... | collective-permute-start | bytes 1572872 | tf_op jit(solution)/shard_map/ppermute | solution.py:282
  60.8 1.6 %copy-start = (bf16[1,1024,1024]{2,1,0:T(8,128)(2,1)S(1)}, bf16[1,1024,1024]{2,1,0:T(8,128)(2,1)}, u32[]{:S(2)}) copy-start(bf16[1,1024,1024]{2,1,0:T(8,128)(2,1)} %param.7) | copy-start | bytes 6291460
  62.4 1.6 %copy-start.1 = (bf16[1,1024,1024]{2,1,0:T(8,128)(2,1)S(1)}, bf16[1,1024,1024]{2,1,0:T(8,128)(2,1)}, u32[]{:S(2)}) copy-start(bf16[1,1024,1024]{2,1,0:T(8,128)(2,1)} %param.8) | copy-start | bytes 6291460
  65.3 26.6 %copy-start.4 = (s32[32,1]{0,1:T(1,128)S(1)}, s32[32,1]{0,1:T(1,128)}, u32[]{:S(2)}) copy-start(s32[32,1]{0,1:T(1,128)} %param.6) | copy-start | bytes 388
  65.3 32.6 %copy-start.2 = (f32[128,1024]{1,0:T(8,128)S(1)}, f32[128,1024]{1,0:T(8,128)}, u32[]{:S(2)}) copy-start(f32[128,1024]{1,0:T(8,128)} %tok_ref.3) | copy-start | bytes 1572868
  65.3 32.6 %copy-start.3 = (f32[128,1024]{1,0:T(8,128)S(1)}, f32[128,1024]{1,0:T(8,128)}, u32[]{:S(2)}) copy-start(f32[128,1024]{1,0:T(8,128)} %up_ref.3) | copy-start | bytes 1572868
  65.3 3.9 %collective-permute-start.1 = (bf16[512,512]{1,0:T(8,128)(2,1)S(1)}, bf16[512,512]{1,0:T(8,128)(2,1)S(1)}, u32[]{:S(2)}, u32[]{:S(2)}) collective-permute-start(bf16[512,512]{1,0:T(8,128)(2,1)S(1)} %get-tuple-element.22), channel_id=1, source_target_pairs={{0,1},{1,0},{2,3},{3,2},{4,5},{5,4},{6,7},{7,6},{8,9},{9,8},{10,11... | collective-permute-start | bytes 1572872 | tf_op jit(solution)/shard_map/ppermute | solution.py:290
  92.3 5.6 %collective-permute-start.2 = (bf16[256,512]{1,0:T(8,128)(2,1)S(1)}, bf16[256,512]{1,0:T(8,128)(2,1)S(1)}, u32[]{:S(2)}, u32[]{:S(2)}) collective-permute-start(bf16[256,512]{1,0:T(8,128)(2,1)S(1)} %home.1.mine_ref), channel_id=1, source_target_pairs={{0,1},{1,0},{2,3},{3,2},{4,5},{5,4},{6,7},{7,6},{8,9},{9,8},{10,11... | collective-permute-start | bytes 786440 | tf_op jit(solution)/shard_map/ppermute | solution.py:298
Sparse Core Ops, SparseCore 0:
  61.0 53.9 reduce-scatter.1

commit v3 on v2

--- a/solution.py
+++ b/solution.py
@@ -73,44 +73,78 @@
         copy.wait()
 
 
-def grads_kernel(
-    block, share, m_ref, mine_ref, other_ref, up_ref, down_ref, part_ref, hid_ref, pg_ref, x_ref, hidt_ref
+def hidden_kernel(
+    block, groups, m_ref, group_ref, mine_ref, other_ref, up_ref, down_ref,
+    far_up_ref, far_down_ref, hid_ref, pg_ref, turned_ref, hidt_ref, x_ref,
 ):
     rows, half_cols = mine_ref.shape
     half = rows // 2
-    hidden_cols = hid_ref.shape[1]
-    step = pl.program_id(0)
-
-    @pl.when(step == 0)
-    def _():
-        first = m_ref[0] == 0
-        mine = mine_ref[...]
-        other = mm(split_rows(rows, block), other_ref[...], NN).astype(BF16)
-        x_ref[:, :half_cols] = jnp.where(first, mine, other)
-        x_ref[:, half_cols:] = jnp.where(first, other, mine)
-        pre = mm(x_ref[:half, :], up_ref[...], NN)
-        hidden_grad = mm(x_ref[half:, :], down_ref[...], NT)
-        square = pre * pre
-        t = jnp.tanh(GELU_C * (pre + GELU_A * (square * pre)))
-        cdf = 0.5 * (1.0 + t)
-        slope = cdf + 0.5 * pre * (1.0 - t * t) * (GELU_C * (1.0 + 3.0 * GELU_A * square))
-        hidden = (pre * cdf).astype(BF16)
-        hid_ref[...] = hidden
-        hidt_ref[...] = hidden.T
-        pg_ref[...] = (hidden_grad * slope).astype(BF16)
-
-    shares = part_ref.shape[0] // (2 * hidden_cols)
-    span = shares * share
-    cols = pl.ds(pl.multiple_of(step * span, span), span)
-    up_part = mm(x_ref[:half, cols], pg_ref[...], TN).astype(BF16)
-    down_part = mm(hidt_ref[...], x_ref[half:, cols], NN).astype(BF16)
-    for k in range(shares):
-        own = slice(k * share, (k + 1) * share)
-        base = 2 * k * hidden_cols
-        for j in range(hidden_cols // share):
-            at = slice(j * share, (j + 1) * share)
-            part_ref[base + j * share : base + (j + 1) * share, :] = up_part[own, at]
-        part_ref[base + hidden_cols : base + 2 * hidden_cols, :] = down_part[:, own]
+    share = turned_ref.shape[1] // groups
+    first = m_ref[0] == 0
+    mine = mine_ref[...]
+    other = mm(split_rows(rows, block), other_ref[...], NN).astype(BF16)
+    x_ref[:, :half_cols] = jnp.where(first, mine, other)
+    x_ref[:, half_cols:] = jnp.where(first, other, mine)
+    for k in range(groups):
+        owner = lax.rem(group_ref[0] + k, groups)
+        turned_ref[:, k * share : (k + 1) * share] = x_ref[:, pl.ds(pl.multiple_of(owner * share, share), share)]
+    pre = mm(x_ref[:half, :], up_ref[...], NN)
+    hidden_grad = mm(x_ref[half:, :], down_ref[...], NT)
+    square = pre * pre
+    t = jnp.tanh(GELU_C * (pre + GELU_A * (square * pre)))
+    cdf = 0.5 * (1.0 + t)
+    slope = cdf + 0.5 * pre * (1.0 - t * t) * (GELU_C * (1.0 + 3.0 * GELU_A * square))
+    hidden = (pre * cdf).astype(BF16)
+    hid_ref[...] = hidden
+    hidt_ref[...] = hidden.T
+    pg_ref[...] = (hidden_grad * slope).astype(BF16)
+    far = slice(groups // 2 * share, (groups // 2 + 1) * share)
+    up_share(far_up_ref, 0, mm(turned_ref[:half, far], pg_ref[...], TN).astype(BF16))
+    far_down_ref[...] = mm(hidt_ref[...], turned_ref[half:, far], NN).astype(BF16)
+
+
+def up_share(ref, base, value):
+    share = value.shape[0]
+    for j in range(value.shape[1] // share):
+        ref[base + j * share : base + (j + 1) * share, :] = value[:, j * share : (j + 1) * share]
+
+
+def shares_kernel(slots, turned_ref, hidt_ref, pg_ref, *part_refs):
+    half = pg_ref.shape[0]
+    hidden_cols, share = hidt_ref.shape[0], part_refs[0].shape[1]
+    done = 0
+    for first, last in slots:
+        cols = slice(first * share, last * share)
+        up_part = mm(turned_ref[:half, cols], pg_ref[...], TN).astype(BF16)
+        down_part = mm(hidt_ref[...], turned_ref[half:, cols], NN).astype(BF16)
+        for k in range(last - first):
+            own = slice(k * share, (k + 1) * share)
+            up_share(part_refs[done], 0, up_part[own, :])
+            part_refs[done][hidden_cols:, :] = down_part[:, own]
+            done += 1
+
+
+def hop_kernel(lower, got_ref, part_ref, out_ref):
+    half = out_ref.shape[0] // 2
+    if lower is None:
+        out_ref[...] = (part_ref[...].astype(F32) + got_ref[...].astype(F32)).astype(BF16)
+        return
+    came = slice(half, 2 * half) if lower else slice(0, half)
+    fresh = slice(0, half) if lower else slice(half, 2 * half)
+    out_ref[came, :] = (part_ref[came, :].astype(F32) + got_ref[...].astype(F32)).astype(BF16)
+    out_ref[fresh, :] = part_ref[fresh, :]
+
+
+def last_kernel(left_ref, right_ref, part_ref, up_ref, down_ref):
+    hidden_cols, share = down_ref.shape
+
+    def total(at):
+        return part_ref[at, :].astype(F32) + (left_ref[at, :].astype(F32) + right_ref[at, :].astype(F32))
+
+    for j in range(hidden_cols // share):
+        at = slice(j * share, (j + 1) * share)
+        up_ref[:, at] = total(at)
+    down_ref[...] = total(slice(hidden_cols, 2 * hidden_cols))
 
 
 def returns_kernel(m_ref, hid_ref, pg_ref, up_ref, down_ref, keep_ref, send_ref):
@@ -158,15 +192,7 @@
     grad_ref[:, half_cols:] = up_ref[:, half_cols:] + high[rows:]
 
 
-def unpack_kernel(part_ref, up_ref, down_ref):
-    hidden_cols, share = down_ref.shape
-    for j in range(hidden_cols // share):
-        at = slice(j * share, (j + 1) * share)
-        up_ref[:, at] = part_ref[at, :].astype(F32)
-    down_ref[...] = part_ref[hidden_cols:, :].astype(F32)
-
-
-PARAMS = pltpu.CompilerParams(vmem_limit_bytes=20 * 2**20)
+PARAMS = pltpu.CompilerParams(vmem_limit_bytes=16 * 2**20)
 ONCHIP = pl.BlockSpec(memory_space=pltpu.VMEM)
 
 
@@ -233,29 +259,48 @@
     )(onchip(mine), offchip(up_matrix), offchip(down_matrix))
 
 
-def grads_call(block, groups, m, mine, other, up_matrix, down_matrix):
+def weight_grads(block, groups, m, group, mine, other, up_matrix, down_matrix):
     rows = mine.shape[0]
     width, hidden_cols = up_matrix.shape
     share = width // groups
-    steps = max(1, groups // 4)
-    half_shape = pltpu.VMEM((rows // 2, hidden_cols), BF16)
-    return pl.pallas_call(
-        functools.partial(grads_kernel, block, share),
-        out_shape=(pltpu.HBM((2 * hidden_cols * groups, share), BF16), half_shape, half_shape),
-        grid_spec=pltpu.PrefetchScalarGridSpec(
-            num_scalar_prefetch=1,
-            grid=(steps,),
-            in_specs=[ONCHIP] * 4,
-            out_specs=(
-                pl.BlockSpec((2 * hidden_cols * groups // steps, share), lambda i, m_ref: (i, 0)),
-                ONCHIP,
-                ONCHIP,
-            ),
-            scratch_shapes=[pltpu.VMEM((rows, width), BF16), pltpu.VMEM((hidden_cols, rows // 2), BF16)],
+    half = groups // 2
+    vmem = pltpu.VMEM
+    far_up, far_down, hidden, pre_grad, turned, hidden_t = pl.pallas_call(
+        functools.partial(hidden_kernel, block, groups),
+        out_shape=(
+            vmem((hidden_cols, share), BF16),
+            vmem((hidden_cols, share), BF16),
+            vmem((rows // 2, hidden_cols), BF16),
+            vmem((rows // 2, hidden_cols), BF16),
+            vmem((rows, width), BF16),
+            vmem((hidden_cols, rows // 2), BF16),
         ),
+        in_specs=[pl.BlockSpec(memory_space=pltpu.SMEM)] * 2 + [ONCHIP] * 4,
+        out_specs=(ONCHIP,) * 6,
+        scratch_shapes=[vmem((rows, width), BF16)],
         compiler_params=PARAMS,
-        name="grads",
-    )(m, onchip(mine), onchip(other), onchip(up_matrix), onchip(down_matrix))
+        name="hidden",
+    )(m, group, onchip(mine), onchip(other), onchip(up_matrix), onchip(down_matrix))
+    ahead = [(i, (i + 1) % groups) for i in range(groups)]
+    behind = [(i, (i - 1) % groups) for i in range(groups)]
+    right = lax.ppermute(far_up, "dp", ahead)
+    left = lax.ppermute(far_down, "dp", behind)
+    size = vmem((2 * hidden_cols, share), BF16)
+    runs = ((0, half), (half + 1, groups))
+    parts = call(functools.partial(shares_kernel, runs), (size,) * (groups - 1), 0, "shares")(
+        onchip(turned), onchip(hidden_t), onchip(pre_grad)
+    )
+    parts = parts[:half] + (None,) + parts[half:]
+    for hop in range(half - 1, 0, -1):
+        whole = hop < half - 1
+        step = call(functools.partial(hop_kernel, None if whole else False), size, 0, "ahead")
+        right = lax.ppermute(step(onchip(right), onchip(parts[hop])), "dp", ahead)
+        step = call(functools.partial(hop_kernel, None if whole else True), size, 0, "behind")
+        left = lax.ppermute(step(onchip(left), onchip(parts[groups - hop])), "dp", behind)
+    grad_up, grad_down = call(
+        last_kernel, (shape((share, hidden_cols), F32), shape((hidden_cols, share), F32)), 0, "last"
+    )(onchip(left), onchip(right), onchip(parts[0]))
+    return grad_up, grad_down, hidden, pre_grad
 
 
 def body(tokens, block_experts, weight_up, weight_down, upstream):
@@ -265,9 +310,7 @@
     tok_rows, width = tokens.shape
     block = tok_rows // blocks_dev
     half_cols = width // 2
-    hidden_cols = weight_up.shape[2]
     rows = 2 * experts * block
-    share = width // groups
     m = lax.axis_index("mp").astype(jnp.int32).reshape(1)
     labels = block_experts.reshape(1, blocks_dev)
     swap = [(0, 1), (1, 0)]
@@ -281,12 +324,12 @@
     arrived = exchange(slots)
     other = lax.ppermute(arrived, "mp", swap)
     mine, up_matrix, down_matrix = front_call(block, arrived, weight_up[0], weight_down[0])
-    parts, hidden, pre_grad = grads_call(block, groups, m, mine, other, up_matrix, down_matrix)
-    summed = lax.psum_scatter(parts, "dp", scatter_dimension=0, tiled=True)
+    group = lax.axis_index("dp").astype(jnp.int32).reshape(1)
+    grad_up, grad_down, hidden, pre_grad = weight_grads(block, groups, m, group, mine, other, up_matrix, down_matrix)
 
     keep, send = call(
         returns_kernel, (pltpu.VMEM((rows, half_cols), F32), pltpu.VMEM((rows, half_cols), BF16)), 1, "returns"
-    )(m, onchip(hidden), onchip(pre_grad), weight_up[0], weight_down[0])
+    )(m, onchip(hidden), onchip(pre_grad), onchip(up_matrix), onchip(down_matrix))
     got = lax.ppermute(send, "mp", swap)
     added = call(functools.partial(add_kernel, block), pltpu.VMEM((rows, half_cols), BF16), 0, "add")(
         onchip(keep), onchip(got)
@@ -299,9 +342,6 @@
     layer_output, grad_tokens = call(
         final_kernel, (shape(tokens.shape, F32), shape(tokens.shape, F32)), 1, "final"
     )(m, onchip(home), onchip(home_other), tokens, upstream)
-    grad_up, grad_down = call(
-        unpack_kernel, (shape((share, hidden_cols), F32), shape((hidden_cols, share), F32)), 0, "unpack"
-    )(offchip(summed))
     return (layer_output, grad_tokens, grad_up[None], grad_down[None])
 
 

time: 124 us -> 122 us (0.984)
  the two profiles are of different devices: /device:TPU:1 before, /device:TPU:52 now
where the time goes in v3:
time: 122 us
  blocking collectives  41.9 us (34%)
  starting transfers between devices  40.2 us (33%)
  waiting for transfers between devices  20.1 us (16%)
  Pallas kernels  18.5 us (15%)
    all_to_all x1, blocking collectives, exchange(): lax.all_to_all(shaped, 'expert', split_axis=0, concat_axis=0, tiled=True)  41.9 us
    ppermute x3, starting transfers between devices, weight_grads(): right = lax.ppermute(step(onchip(right), onchip(parts[hop])), 'dp', ahead)  16.4 us
    ppermute x3, waiting for transfers between devices, weight_grads(): right = lax.ppermute(step(onchip(right), onchip(parts[hop])), 'dp', ahead)  12.2 us
    pallas_call x12, Pallas kernels, run(): pl.pallas_call(kernel, out_shape=outs, in_specs=[pl.BlockSpec(memory_spac...  12.2 us
    ppermute x3, waiting for transfers between devices, weight_grads(): lax.ppermute(step(onchip(left), onchip(parts[groups - hop])), 'dp', behind)  6.44 us
    ppermute x3, starting transfers between devices, weight_grads(): lax.ppermute(step(onchip(left), onchip(parts[groups - hop])), 'dp', behind)  5.87 us
    all_to_all x1, starting transfers between devices, exchange(): lax.all_to_all(shaped, 'expert', split_axis=0, concat_axis=0, tiled=True)  5.22 us
    ppermute x1, starting transfers between devices, weight_grads(): right = lax.ppermute(far_up, 'dp', ahead)  4.82 us
  transfers between devices with their start and end apart: 12, of which 6 were waited for; matrix products, arithmetic and copies ran while one was open for 0% of the time, Pallas kernels for 11%

profile of v3, /device:TPU:52, one launch (start us, length us, event | category | flops | bytes accessed | tf_op | source)
XLA Modules:
  0.0 121.5 jit_solution(10866515995177540229)
XLA Ops:
  0.6 1.6 %slots.1 = bf16[512,512]{1,0:T(8,128)(2,1)S(1)} custom-call(s32[1]{0:T(128)} %bitcast.m_ref, s32[1,32]{1,0:T(1,128)} %bitcast.15, f32[128,1024]{1,0:T(8,128)} %tok_ref.3, f32[128,1024]{1,0:T(8,128)} %up_ref.3), custom_call_target="tpu_custom_call" | custom-call | tf_op jit(solution)/shard_map/slots/pallas_call | solution.py:231
  2.2 41.9 %all_to_all.10 = bf16[64,8,512]{2,1,0:T(8,128)(2,1)S(1)} all-to-all(bf16[64,8,512]{2,1,0:T(8,128)(2,1)S(1)} %bitcast.14), channel_id=1, replica_groups=mesh['dp'=8,'expert'=64,'mp'=2] {'expert'}, dimensions={0} | all-to-all | bytes 1048576 | tf_op jit(solution)/shard_map/all_to_all | solution.py:320
  44.1 1.9 %collective-permute-start = (bf16[512,512]{1,0:T(8,128)(2,1)S(1)}, bf16[512,512]{1,0:T(8,128)(2,1)S(1)}, u32[]{:S(2)}, u32[]{:S(2)}) collective-permute-start(bf16[512,512]{1,0:T(8,128)(2,1)S(1)} %bitcast.11), channel_id=1, source_target_pairs={{0,1},{1,0},{2,3},{3,2},{4,5},{5,4},{6,7},{7,6},{8,9},{9,8},{10,11... | collective-permute-start | bytes 1572872 | tf_op jit(solution)/shard_map/ppermute | solution.py:325
  46.0 2.3 %front.1 = (bf16[512,512]{1,0:T(8,128)(2,1)S(1)}, bf16[1024,1024]{1,0:T(8,128)(2,1)S(1)}, bf16[1024,1024]{1,0:T(8,128)(2,1)S(1)}) custom-call(bf16[512,512]{1,0:T(8,128)(2,1)S(1)} %bitcast.12, bf16[1024,1024]{1,0:T(8,128)(2,1)} %bitcast.17, bf16[1024,1024]{1,0:T(8,128)(2,1)} %bitcast.18), custom_call_target="tpu_custom_call" | custom-call | tf_op jit(solution)/shard_map/front/pallas_call | solution.py:247
  48.3 2.5 %hidden.1 = (bf16[1024,128]{1,0:T(8,128)(2,1)S(1)}, bf16[1024,128]{1,0:T(8,128)(2,1)S(1)}, bf16[256,1024]{1,0:T(8,128)(2,1)S(1)}, bf16[256,1024]{1,0:T(8,128)(2,...) custom-call(s32[1]{0:T(128)} %bitcast.m_ref, s32[1]{0:T(128)} %bitcast.2.group_ref, ...), custom_call_target="tpu_custom_call" | custom-call | tf_op jit(solution)/shard_map/hidden/pallas_call | solution.py:268
  50.8 4.8 %collective-permute-start.7 = (bf16[1024,128]{1,0:T(8,128)(2,1)S(1)}, bf16[1024,128]{1,0:T(8,128)(2,1)S(1)}, u32[]{:S(2)}, u32[]{:S(2)}) collective-permute-start(bf16[1024,128]{1,0:T(8,128)(2,1)S(1)} %get-tuple-element.41), channel_id=1, source_target_pairs={{0,128},{128,256},{256,384},{384,512},{512,640},{640,768},{768,896... | collective-permute-start | bytes 786440 | tf_op jit(solution)/shard_map/ppermute | solution.py:286
  55.6 1.9 %collective-permute-start.3 = (bf16[1024,128]{1,0:T(8,128)(2,1)S(1)}, bf16[1024,128]{1,0:T(8,128)(2,1)S(1)}, u32[]{:S(2)}, u32[]{:S(2)}) collective-permute-start(bf16[1024,128]{1,0:T(8,128)(2,1)S(1)} %get-tuple-element.35), channel_id=1, source_target_pairs={{0,896},{128,0},{256,128},{384,256},{512,384},{640,512},{768,640},... | collective-permute-start | bytes 786440 | tf_op jit(solution)/shard_map/ppermute | solution.py:287
  57.5 1.3 %returns.1 = (f32[512,512]{1,0:T(8,128)S(1)}, bf16[512,512]{1,0:T(8,128)(2,1)S(1)}) custom-call(s32[1]{0:T(128)} %bitcast.m_ref, bf16[256,1024]{1,0:T(8,128)(2,1)S(1)} %get-tuple-element.29.hid_ref, bf16[256,1024]{1,0:T(8,128)(2,1)S(1)} %get-tuple-element.30.pg_ref, bf16[1024,1024]{1,0:T(8,128)(2,1)S(1)} %get-tuple-element.27.up_ref, ...), custom_call_target="tpu_custom_call" | custom-call | tf_op jit(solution)/shard_map/returns/pallas_call | solution.py:212
  58.8 2.1 %collective-permute-start.1 = (bf16[512,512]{1,0:T(8,128)(2,1)S(1)}, bf16[512,512]{1,0:T(8,128)(2,1)S(1)}, u32[]{:S(2)}, u32[]{:S(2)}) collective-permute-start(bf16[512,512]{1,0:T(8,128)(2,1)S(1)} %get-tuple-element.32), channel_id=1, source_target_pairs={{0,1},{1,0},{2,3},{3,2},{4,5},{5,4},{6,7},{7,6},{8,9},{9,8},{10,11... | collective-permute-start | bytes 1572872 | tf_op jit(solution)/shard_map/ppermute | solution.py:333
  60.9 1.2 %shares.1 = (bf16[2048,128]{1,0:T(8,128)(2,1)S(1)}, bf16[2048,128]{1,0:T(8,128)(2,1)S(1)}, bf16[2048,128]{1,0:T(8,128)(2,1)S(1)}, bf16[2048,128]{1,0:T(8,128)(2,...) custom-call(bf16[512,1024]{1,0:T(8,128)(2,1)S(1)} %get-tuple-element.36.turned_r, ...), custom_call_target="tpu_custom_call" | custom-call | tf_op jit(solution)/shard_map/shares/pallas_call | solution.py:212
  62.2 0.9 ahead.3
  63.0 5.2 %collective-permute-start.8 = (bf16[2048,128]{1,0:T(8,128)(2,1)}, bf16[2048,128]{1,0:T(8,128)(2,1)}, u32[]{:S(2)}, u32[]{:S(2)}) collective-permute-start(bf16[2048,128]{1,0:T(8,128)(2,1)} %ahead.3), channel_id=1, source_target_pairs={{0,128},{128,256},{256,384},{384,512},{512,640},{640,768},{768,896... | collective-permute-start | bytes 1572872 | tf_op jit(solution)/shard_map/ppermute | solution.py:297
  68.3 0.9 behind.3
  69.1 1.9 %collective-permute-start.4 = (bf16[2048,128]{1,0:T(8,128)(2,1)}, bf16[2048,128]{1,0:T(8,128)(2,1)}, u32[]{:S(2)}, u32[]{:S(2)}) collective-permute-start(bf16[2048,128]{1,0:T(8,128)(2,1)} %behind.3), channel_id=1, source_target_pairs={{0,896},{128,0},{256,128},{384,256},{512,384},{640,512},{768,640},... | collective-permute-start | bytes 1572872 | tf_op jit(solution)/shard_map/ppermute | solution.py:299
  71.0 1.3 %add.1 = bf16[512,512]{1,0:T(8,128)(2,1)} custom-call(f32[512,512]{1,0:T(8,128)S(1)} %get-tuple-element.31.keep_ref, bf16[512,512]{1,0:T(8,128)(2,1)S(1)} %collective-permute-done.1.got_ref), custom_call_target="tpu_custom_call" | custom-call | tf_op jit(solution)/shard_map/add/pallas_call | solution.py:212
  72.3 5.2 %all-to-all-start.1 = ((bf16[64,8,512]{2,1,0:T(8,128)(2,1)}), bf16[64,8,512]{2,1,0:T(8,128)(2,1)S(1)}, u32[]{:S(2)}, u32[]{:S(2)}) async-start(bf16[64,8,512]{2,1,0:T(8,128)(2,1)} %bitcast.7), calls=%async_computation.1 | async-start | bytes 1048576 | tf_op jit(solution)/shard_map/all_to_all | solution.py:320
  77.5 2.5 %collective-permute-done.8.got_ref = bf16[2048,128]{1,0:T(8,128)(2,1)} collective-permute-done((bf16[2048,128]{1,0:T(8,128)(2,1)}, bf16[2048,128]{1,0:T(8,128)(2,1)}, u32[]{:S(2)}, u32[]{:S(2)}) %collective-permute-start.8) | collective-permute-done | bytes 524320 | tf_op jit(solution)/shard_map/ppermute | solution.py:297
  80.1 1.2 ahead.4
  81.3 5.6 %collective-permute-start.9 = (bf16[2048,128]{1,0:T(8,128)(2,1)S(1)}, bf16[2048,128]{1,0:T(8,128)(2,1)S(1)}, u32[]{:S(2)}, u32[]{:S(2)}) collective-permute-start(bf16[2048,128]{1,0:T(8,128)(2,1)S(1)} %ahead.4), channel_id=1, source_target_pairs={{0,128},{128,256},{256,384},{384,512},{512,640},{640,768},{768,896... | collective-permute-start | bytes 1572872 | tf_op jit(solution)/shard_map/ppermute | solution.py:297
  86.9 1.2 behind.4
  88.1 2.1 %collective-permute-start.5 = (bf16[2048,128]{1,0:T(8,128)(2,1)S(1)}, bf16[2048,128]{1,0:T(8,128)(2,1)S(1)}, u32[]{:S(2)}, u32[]{:S(2)}) collective-permute-start(bf16[2048,128]{1,0:T(8,128)(2,1)S(1)} %behind.4), channel_id=1, source_target_pairs={{0,896},{128,0},{256,128},{384,256},{512,384},{640,512},{768,640},... | collective-permute-start | bytes 1572872 | tf_op jit(solution)/shard_map/ppermute | solution.py:299
  90.1 7.4 %collective-permute-done.9.got_ref = bf16[2048,128]{1,0:T(8,128)(2,1)S(1)} collective-permute-done((bf16[2048,128]{1,0:T(8,128)(2,1)S(1)}, bf16[2048,128]{1,0:T(8,128)(2,1)S(1)}, u32[]{:S(2)}, u32[]{:S(2)}) %collective-permute-start.9) | collective-permute-done | bytes 524320 | tf_op jit(solution)/shard_map/ppermute | solution.py:297
  97.6 0.9 ahead.5
  98.5 5.6 %collective-permute-start.10 = (bf16[2048,128]{1,0:T(8,128)(2,1)}, bf16[2048,128]{1,0:T(8,128)(2,1)S(1)}, u32[]{:S(2)}, u32[]{:S(2)}) collective-permute-start(bf16[2048,128]{1,0:T(8,128)(2,1)} %ahead.5), channel_id=1, source_target_pairs={{0,128},{128,256},{256,384},{384,512},{512,640},{640,768},{768,896... | collective-permute-start | bytes 1572872 | tf_op jit(solution)/shard_map/ppermute | solution.py:297
  104.2 0.9 behind.5
  105.2 1.9 %collective-permute-start.6 = (bf16[2048,128]{1,0:T(8,128)(2,1)}, bf16[2048,128]{1,0:T(8,128)(2,1)S(1)}, u32[]{:S(2)}, u32[]{:S(2)}) collective-permute-start(bf16[2048,128]{1,0:T(8,128)(2,1)} %behind.5), channel_id=1, source_target_pairs={{0,896},{128,0},{256,128},{384,256},{512,384},{640,512},{768,640},... | collective-permute-start | bytes 1572872 | tf_op jit(solution)/shard_map/ppermute | solution.py:299
  107.5 1.9 %collective-permute-start.2 = (bf16[256,512]{1,0:T(8,128)(2,1)S(1)}, bf16[256,512]{1,0:T(8,128)(2,1)S(1)}, u32[]{:S(2)}, u32[]{:S(2)}) collective-permute-start(bf16[256,512]{1,0:T(8,128)(2,1)S(1)} %home.1.mine_ref), channel_id=1, source_target_pairs={{0,1},{1,0},{2,3},{3,2},{4,5},{5,4},{6,7},{7,6},{8,9},{9,8},{10,11... | collective-permute-start | bytes 786440 | tf_op jit(solution)/shard_map/ppermute | solution.py:341
  109.4 1.5 %collective-permute-done.2.other_ref = bf16[256,512]{1,0:T(8,128)(2,1)S(1)} collective-permute-done((bf16[256,512]{1,0:T(8,128)(2,1)S(1)}, bf16[256,512]{1,0:T(8,128)(2,1)S(1)}, u32[]{:S(2)}, u32[]{:S(2)}) %collective-permute-start.2) | collective-permute-done | bytes 262176 | tf_op jit(solution)/shard_map/ppermute | solution.py:341
  110.9 1.0 final.1
  112.0 2.2 %collective-permute-done.10.right_ref = bf16[2048,128]{1,0:T(8,128)(2,1)S(1)} collective-permute-done((bf16[2048,128]{1,0:T(8,128)(2,1)}, bf16[2048,128]{1,0:T(8,128)(2,1)S(1)}, u32[]{:S(2)}, u32[]{:S(2)}) %collective-permute-start.10) | collective-permute-done | bytes 524320 | tf_op jit(solution)/shard_map/ppermute | solution.py:297
  114.2 6.3 %collective-permute-done.6.left_ref = bf16[2048,128]{1,0:T(8,128)(2,1)S(1)} collective-permute-done((bf16[2048,128]{1,0:T(8,128)(2,1)}, bf16[2048,128]{1,0:T(8,128)(2,1)S(1)}, u32[]{:S(2)}, u32[]{:S(2)}) %collective-permute-start.6) | collective-permute-done | bytes 524320 | tf_op jit(solution)/shard_map/ppermute | solution.py:299
  120.5 1.1 last.1
  (14 shorter events, 0.6 us)
Async XLA Ops:
  44.1 4.2 %collective-permute-start = (bf16[512,512]{1,0:T(8,128)(2,1)S(1)}, bf16[512,512]{1,0:T(8,128)(2,1)S(1)}, u32[]{:S(2)}, u32[]{:S(2)}) collective-permute-start(bf16[512,512]{1,0:T(8,128)(2,1)S(1)} %bitcast.11), channel_id=1, source_target_pairs={{0,1},{1,0},{2,3},{3,2},{4,5},{5,4},{6,7},{7,6},{8,9},{9,8},{10,11... | collective-permute-start | bytes 1572872 | tf_op jit(solution)/shard_map/ppermute | solution.py:325
  50.8 11.4 %collective-permute-start.7 = (bf16[1024,128]{1,0:T(8,128)(2,1)S(1)}, bf16[1024,128]{1,0:T(8,128)(2,1)S(1)}, u32[]{:S(2)}, u32[]{:S(2)}) collective-permute-start(bf16[1024,128]{1,0:T(8,128)(2,1)S(1)} %get-tuple-element.41), channel_id=1, source_target_pairs={{0,128},{128,256},{256,384},{384,512},{512,640},{640,768},{768,896... | collective-permute-start | bytes 786440 | tf_op jit(solution)/shard_map/ppermute | solution.py:286
  55.6 12.7 %collective-permute-start.3 = (bf16[1024,128]{1,0:T(8,128)(2,1)S(1)}, bf16[1024,128]{1,0:T(8,128)(2,1)S(1)}, u32[]{:S(2)}, u32[]{:S(2)}) collective-permute-start(bf16[1024,128]{1,0:T(8,128)(2,1)S(1)} %get-tuple-element.35), channel_id=1, source_target_pairs={{0,896},{128,0},{256,128},{384,256},{512,384},{640,512},{768,640},... | collective-permute-start | bytes 786440 | tf_op jit(solution)/shard_map/ppermute | solution.py:287
  58.8 12.3 %collective-permute-start.1 = (bf16[512,512]{1,0:T(8,128)(2,1)S(1)}, bf16[512,512]{1,0:T(8,128)(2,1)S(1)}, u32[]{:S(2)}, u32[]{:S(2)}) collective-permute-start(bf16[512,512]{1,0:T(8,128)(2,1)S(1)} %get-tuple-element.32), channel_id=1, source_target_pairs={{0,1},{1,0},{2,3},{3,2},{4,5},{5,4},{6,7},{7,6},{8,9},{9,8},{10,11... | collective-permute-start | bytes 1572872 | tf_op jit(solution)/shard_map/ppermute | solution.py:333
  63.0 17.1 %collective-permute-start.8 = (bf16[2048,128]{1,0:T(8,128)(2,1)}, bf16[2048,128]{1,0:T(8,128)(2,1)}, u32[]{:S(2)}, u32[]{:S(2)}) collective-permute-start(bf16[2048,128]{1,0:T(8,128)(2,1)} %ahead.3), channel_id=1, source_target_pairs={{0,128},{128,256},{256,384},{384,512},{512,640},{640,768},{768,896... | collective-permute-start | bytes 1572872 | tf_op jit(solution)/shard_map/ppermute | solution.py:297
  69.1 17.7 %collective-permute-start.4 = (bf16[2048,128]{1,0:T(8,128)(2,1)}, bf16[2048,128]{1,0:T(8,128)(2,1)}, u32[]{:S(2)}, u32[]{:S(2)}) collective-permute-start(bf16[2048,128]{1,0:T(8,128)(2,1)} %behind.3), channel_id=1, source_target_pairs={{0,896},{128,0},{256,128},{384,256},{512,384},{640,512},{768,640},... | collective-permute-start | bytes 1572872 | tf_op jit(solution)/shard_map/ppermute | solution.py:299
  72.3 34.8 %all-to-all-start.1 = ((bf16[64,8,512]{2,1,0:T(8,128)(2,1)}), bf16[64,8,512]{2,1,0:T(8,128)(2,1)S(1)}, u32[]{:S(2)}, u32[]{:S(2)}) async-start(bf16[64,8,512]{2,1,0:T(8,128)(2,1)} %bitcast.7), calls=%async_computation.1 | async-start | bytes 1048576 | tf_op jit(solution)/shard_map/all_to_all | solution.py:320
  81.3 16.3 %collective-permute-start.9 = (bf16[2048,128]{1,0:T(8,128)(2,1)S(1)}, bf16[2048,128]{1,0:T(8,128)(2,1)S(1)}, u32[]{:S(2)}, u32[]{:S(2)}) collective-permute-start(bf16[2048,128]{1,0:T(8,128)(2,1)S(1)} %ahead.4), channel_id=1, source_target_pairs={{0,128},{128,256},{256,384},{384,512},{512,640},{640,768},{768,896... | collective-permute-start | bytes 1572872 | tf_op jit(solution)/shard_map/ppermute | solution.py:297
  86.9 20.2 %copy-start.2 = (s32[32,1]{0,1:T(1,128)S(1)}, s32[32,1]{0,1:T(1,128)}, u32[]{:S(2)}) copy-start(s32[32,1]{0,1:T(1,128)} %param.6) | copy-start | bytes 388
  88.1 22.9 %copy-start = (f32[128,1024]{1,0:T(8,128)S(1)}, f32[128,1024]{1,0:T(8,128)}, u32[]{:S(2)}) copy-start(f32[128,1024]{1,0:T(8,128)} %tok_ref.3) | copy-start | bytes 1572868
  88.1 22.9 %copy-start.1 = (f32[128,1024]{1,0:T(8,128)S(1)}, f32[128,1024]{1,0:T(8,128)}, u32[]{:S(2)}) copy-start(f32[128,1024]{1,0:T(8,128)} %up_ref.3) | copy-start | bytes 1572868
  88.1 16.2 %collective-permute-start.5 = (bf16[2048,128]{1,0:T(8,128)(2,1)S(1)}, bf16[2048,128]{1,0:T(8,128)(2,1)S(1)}, u32[]{:S(2)}, u32[]{:S(2)}) collective-permute-start(bf16[2048,128]{1,0:T(8,128)(2,1)S(1)} %behind.4), channel_id=1, source_target_pairs={{0,896},{128,0},{256,128},{384,256},{512,384},{640,512},{768,640},... | collective-permute-start | bytes 1572872 | tf_op jit(solution)/shard_map/ppermute | solution.py:299
  98.5 15.7 %collective-permute-start.10 = (bf16[2048,128]{1,0:T(8,128)(2,1)}, bf16[2048,128]{1,0:T(8,128)(2,1)S(1)}, u32[]{:S(2)}, u32[]{:S(2)}) collective-permute-start(bf16[2048,128]{1,0:T(8,128)(2,1)} %ahead.5), channel_id=1, source_target_pairs={{0,128},{128,256},{256,384},{384,512},{512,640},{640,768},{768,896... | collective-permute-start | bytes 1572872 | tf_op jit(solution)/shard_map/ppermute | solution.py:297
  105.2 15.3 %collective-permute-start.6 = (bf16[2048,128]{1,0:T(8,128)(2,1)}, bf16[2048,128]{1,0:T(8,128)(2,1)S(1)}, u32[]{:S(2)}, u32[]{:S(2)}) collective-permute-start(bf16[2048,128]{1,0:T(8,128)(2,1)} %behind.5), channel_id=1, source_target_pairs={{0,896},{128,0},{256,128},{384,256},{512,384},{640,512},{768,640},... | collective-permute-start | bytes 1572872 | tf_op jit(solution)/shard_map/ppermute | solution.py:299
  107.5 3.4 %collective-permute-start.2 = (bf16[256,512]{1,0:T(8,128)(2,1)S(1)}, bf16[256,512]{1,0:T(8,128)(2,1)S(1)}, u32[]{:S(2)}, u32[]{:S(2)}) collective-permute-start(bf16[256,512]{1,0:T(8,128)(2,1)S(1)} %home.1.mine_ref), channel_id=1, source_target_pairs={{0,1},{1,0},{2,3},{3,2},{4,5},{5,4},{6,7},{7,6},{8,9},{9,8},{10,11... | collective-permute-start | bytes 786440 | tf_op jit(solution)/shard_map/ppermute | solution.py:341

commit v4 on v3

--- a/solution.py
+++ b/solution.py
@@ -135,7 +135,8 @@
     out_ref[fresh, :] = part_ref[fresh, :]
 
 
-def last_kernel(left_ref, right_ref, part_ref, up_ref, down_ref):
+def last_kernel(after_ref, left_ref, right_ref, part_ref, up_ref, down_ref):
+    del after_ref
     hidden_cols, share = down_ref.shape
 
     def total(at):
@@ -160,7 +161,8 @@
         send_ref[at, :] = jnp.where(first, high, low).astype(BF16)
 
 
-def add_kernel(block, keep_ref, got_ref, out_ref):
+def add_kernel(block, after_ref, also_ref, keep_ref, got_ref, out_ref):
+    del after_ref, also_ref
     total = (keep_ref[...] + got_ref[...].astype(F32)).astype(BF16)
     out_ref[...] = mm(merge_rows(total.shape[0], block), total, NN).astype(BF16)
 
@@ -193,6 +195,10 @@
 
 
 PARAMS = pltpu.CompilerParams(vmem_limit_bytes=16 * 2**20)
+def long(us):
+    return pl.CostEstimate(flops=us * 1_000_000_000, bytes_accessed=us * 3_000_000, transcendentals=0)
+
+
 ONCHIP = pl.BlockSpec(memory_space=pltpu.VMEM)
 
 
@@ -204,17 +210,19 @@
     return pltpu.with_memory_space_constraint(array, pltpu.HBM)
 
 
-def call(kernel, outs, scalars, name):
+def call(kernel, outs, scalars, name, after=0, cost=None):
     one = not isinstance(outs, tuple)
+    unread = [pl.BlockSpec(memory_space=pl.ANY)] * after
 
     def run(*args):
-        arrays = len(args) - scalars
+        arrays = len(args) - scalars - after
         return pl.pallas_call(
             kernel,
             out_shape=outs,
-            in_specs=[pl.BlockSpec(memory_space=pltpu.SMEM)] * scalars + [ONCHIP] * arrays,
+            in_specs=[pl.BlockSpec(memory_space=pltpu.SMEM)] * scalars + unread + [ONCHIP] * arrays,
             out_specs=ONCHIP if one else (ONCHIP,) * len(outs),
             compiler_params=PARAMS,
+            cost_estimate=cost,
             name=name,
         )(*args)
 
@@ -291,16 +299,20 @@
         onchip(turned), onchip(hidden_t), onchip(pre_grad)
     )
     parts = parts[:half] + (None,) + parts[half:]
+    sent = []
     for hop in range(half - 1, 0, -1):
         whole = hop < half - 1
-        step = call(functools.partial(hop_kernel, None if whole else False), size, 0, "ahead")
-        right = lax.ppermute(step(onchip(right), onchip(parts[hop])), "dp", ahead)
-        step = call(functools.partial(hop_kernel, None if whole else True), size, 0, "behind")
-        left = lax.ppermute(step(onchip(left), onchip(parts[groups - hop])), "dp", behind)
-    grad_up, grad_down = call(
-        last_kernel, (shape((share, hidden_cols), F32), shape((hidden_cols, share), F32)), 0, "last"
-    )(onchip(left), onchip(right), onchip(parts[0]))
-    return grad_up, grad_down, hidden, pre_grad
+        step = call(functools.partial(hop_kernel, None if whole else False), size, 0, "ahead", 0, long(4) if hop == 1 else None)
+        sent.append(step(onchip(right), onchip(parts[hop])))
+        right = lax.ppermute(sent[-1], "dp", ahead)
+        step = call(functools.partial(hop_kernel, None if whole else True), size, 0, "behind", 0, long(2) if hop == 1 else None)
+        sent.append(step(onchip(left), onchip(parts[groups - hop])))
+        left = lax.ppermute(sent[-1], "dp", behind)
+    def finish(after):
+        outs = (shape((share, hidden_cols), F32), shape((hidden_cols, share), F32))
+        return call(last_kernel, outs, 0, "last", 1)(offchip(after), onchip(left), onchip(right), onchip(parts[0]))
+
+    return finish, hidden, pre_grad, sent
 
 
 def body(tokens, block_experts, weight_up, weight_down, upstream):
@@ -325,14 +337,14 @@
     other = lax.ppermute(arrived, "mp", swap)
     mine, up_matrix, down_matrix = front_call(block, arrived, weight_up[0], weight_down[0])
     group = lax.axis_index("dp").astype(jnp.int32).reshape(1)
-    grad_up, grad_down, hidden, pre_grad = weight_grads(block, groups, m, group, mine, other, up_matrix, down_matrix)
+    finish, hidden, pre_grad, sent = weight_grads(block, groups, m, group, mine, other, up_matrix, down_matrix)
 
     keep, send = call(
         returns_kernel, (pltpu.VMEM((rows, half_cols), F32), pltpu.VMEM((rows, half_cols), BF16)), 1, "returns"
     )(m, onchip(hidden), onchip(pre_grad), onchip(up_matrix), onchip(down_matrix))
     got = lax.ppermute(send, "mp", swap)
-    added = call(functools.partial(add_kernel, block), pltpu.VMEM((rows, half_cols), BF16), 0, "add")(
-        onchip(keep), onchip(got)
+    added = call(functools.partial(add_kernel, block), pltpu.VMEM((rows, half_cols), BF16), 0, "add", 2)(
+        sent[2], sent[3], onchip(keep), onchip(got)
     )
     back = exchange(added)
     home = call(functools.partial(home_kernel, block), pltpu.VMEM((2 * tok_rows, half_cols), BF16), 0, "home")(
@@ -342,6 +354,7 @@
     layer_output, grad_tokens = call(
         final_kernel, (shape(tokens.shape, F32), shape(tokens.shape, F32)), 1, "final"
     )(m, onchip(home), onchip(home_other), tokens, upstream)
+    grad_up, grad_down = finish(grad_tokens)
     return (layer_output, grad_tokens, grad_up[None], grad_down[None])
 
 

time: 122 us -> 122 us (level)
  the two profiles are of different devices: /device:TPU:52 before, /device:TPU:4 now
where the time goes in v4:
time: 122 us; the launch traced here: 121 us
  blocking collectives  41.9 us (34%)
  starting transfers between devices  41.7 us (34%)
  waiting for transfers between devices  19.9 us (16%)
  Pallas kernels  16.9 us (14%)
    all_to_all x1, blocking collectives, exchange(): lax.all_to_all(shaped, 'expert', split_axis=0, concat_axis=0, tiled=True)  41.9 us
    ppermute x3, starting transfers between devices, weight_grads(): left = lax.ppermute(sent[-1], 'dp', behind)  16.9 us
    pallas_call x12, Pallas kernels, run(): pl.pallas_call(kernel, out_shape=outs, in_specs=[pl.BlockSpec(memory_spac...  10.6 us
    ppermute x3, waiting for transfers between devices, weight_grads(): left = lax.ppermute(sent[-1], 'dp', behind)  7.4 us
    ppermute x1, starting transfers between devices, weight_grads(): left = lax.ppermute(far_down, 'dp', behind)  6.17 us
    ppermute x3, starting transfers between devices, weight_grads(): right = lax.ppermute(sent[-1], 'dp', ahead)  5.75 us
    all_to_all x1, starting transfers between devices, exchange(): lax.all_to_all(shaped, 'expert', split_axis=0, concat_axis=0, tiled=True)  5.21 us
    all_to_all x1, waiting for transfers between devices, exchange(): lax.all_to_all(shaped, 'expert', split_axis=0, concat_axis=0, tiled=True)  4.88 us
  transfers between devices with their start and end apart: 12, of which 6 were waited for; matrix products, arithmetic and copies ran while one was open for 0% of the time, Pallas kernels for 10%

profile of v4, /device:TPU:4, one launch (start us, length us, event | category | flops | bytes accessed | tf_op | source)
XLA Modules:
  0.0 121.3 jit_solution(111119472595766899)
XLA Ops:
  0.6 1.6 %slots.1 = bf16[512,512]{1,0:T(8,128)(2,1)S(1)} custom-call(s32[1]{0:T(128)} %bitcast.m_ref, s32[1,32]{1,0:T(1,128)} %bitcast.15, f32[128,1024]{1,0:T(8,128)} %tok_ref.3, f32[128,1024]{1,0:T(8,128)} %up_ref.3), custom_call_target="tpu_custom_call" | custom-call | tf_op jit(solution)/shard_map/slots/pallas_call | solution.py:239
  2.2 41.9 %all_to_all.10 = bf16[64,8,512]{2,1,0:T(8,128)(2,1)S(1)} all-to-all(bf16[64,8,512]{2,1,0:T(8,128)(2,1)S(1)} %bitcast.14), channel_id=1, replica_groups=mesh['dp'=8,'expert'=64,'mp'=2] {'expert'}, dimensions={0} | all-to-all | bytes 1048576 | tf_op jit(solution)/shard_map/all_to_all | solution.py:332
  44.1 1.9 %collective-permute-start = (bf16[512,512]{1,0:T(8,128)(2,1)S(1)}, bf16[512,512]{1,0:T(8,128)(2,1)S(1)}, u32[]{:S(2)}, u32[]{:S(2)}) collective-permute-start(bf16[512,512]{1,0:T(8,128)(2,1)S(1)} %bitcast.11), channel_id=1, source_target_pairs={{0,1},{1,0},{2,3},{3,2},{4,5},{5,4},{6,7},{7,6},{8,9},{9,8},{10,11... | collective-permute-start | bytes 1572872 | tf_op jit(solution)/shard_map/ppermute | solution.py:337
  46.0 2.3 %front.1 = (bf16[512,512]{1,0:T(8,128)(2,1)S(1)}, bf16[1024,1024]{1,0:T(8,128)(2,1)S(1)}, bf16[1024,1024]{1,0:T(8,128)(2,1)S(1)}) custom-call(bf16[512,512]{1,0:T(8,128)(2,1)S(1)} %bitcast.12, bf16[1024,1024]{1,0:T(8,128)(2,1)} %bitcast.17, bf16[1024,1024]{1,0:T(8,128)(2,1)} %bitcast.18), custom_call_target="tpu_custom_call" | custom-call | tf_op jit(solution)/shard_map/front/pallas_call | solution.py:255
  48.3 2.5 %hidden.1 = (bf16[1024,128]{1,0:T(8,128)(2,1)S(1)}, bf16[1024,128]{1,0:T(8,128)(2,1)S(1)}, bf16[256,1024]{1,0:T(8,128)(2,1)S(1)}, bf16[256,1024]{1,0:T(8,128)(2,...) custom-call(s32[1]{0:T(128)} %bitcast.m_ref, s32[1]{0:T(128)} %bitcast.2.group_ref, ...), custom_call_target="tpu_custom_call" | custom-call | tf_op jit(solution)/shard_map/hidden/pallas_call | solution.py:276
  50.8 6.2 %collective-permute-start.3 = (bf16[1024,128]{1,0:T(8,128)(2,1)S(1)}, bf16[1024,128]{1,0:T(8,128)(2,1)S(1)}, u32[]{:S(2)}, u32[]{:S(2)}) collective-permute-start(bf16[1024,128]{1,0:T(8,128)(2,1)S(1)} %get-tuple-element.35), channel_id=1, source_target_pairs={{0,896},{128,0},{256,128},{384,256},{512,384},{640,512},{768,640},... | collective-permute-start | bytes 786440 | tf_op jit(solution)/shard_map/ppermute | solution.py:295
  56.9 1.9 %collective-permute-start.1 = (bf16[1024,128]{1,0:T(8,128)(2,1)S(1)}, bf16[1024,128]{1,0:T(8,128)(2,1)S(1)}, u32[]{:S(2)}, u32[]{:S(2)}) collective-permute-start(bf16[1024,128]{1,0:T(8,128)(2,1)S(1)} %get-tuple-element.29), channel_id=1, source_target_pairs={{0,128},{128,256},{256,384},{384,512},{512,640},{640,768},{768,896... | collective-permute-start | bytes 786440 | tf_op jit(solution)/shard_map/ppermute | solution.py:294
  58.9 1.2 %shares.1 = (bf16[2048,128]{1,0:T(8,128)(2,1)S(1)}, bf16[2048,128]{1,0:T(8,128)(2,1)S(1)}, bf16[2048,128]{1,0:T(8,128)(2,1)S(1)}, bf16[2048,128]{1,0:T(8,128)(2,...) custom-call(bf16[512,1024]{1,0:T(8,128)(2,1)S(1)} %get-tuple-element.30.turned_r, ...), custom_call_target="tpu_custom_call" | custom-call | tf_op jit(solution)/shard_map/shares/pallas_call | solution.py:219
  60.1 3.0 %collective-permute-done.3.got_ref = bf16[1024,128]{1,0:T(8,128)(2,1)S(1)} collective-permute-done((bf16[1024,128]{1,0:T(8,128)(2,1)S(1)}, bf16[1024,128]{1,0:T(8,128)(2,1)S(1)}, u32[]{:S(2)}, u32[]{:S(2)}) %collective-permute-start.3) | collective-permute-done | bytes 262176 | tf_op jit(solution)/shard_map/ppermute | solution.py:295
  63.2 5.6 %collective-permute-start.4 = (bf16[2048,128]{1,0:T(8,128)(2,1)S(1)}, bf16[2048,128]{1,0:T(8,128)(2,1)S(1)}, u32[]{:S(2)}, u32[]{:S(2)}) collective-permute-start(bf16[2048,128]{1,0:T(8,128)(2,1)S(1)} %behind.3), channel_id=1, source_target_pairs={{0,896},{128,0},{256,128},{384,256},{512,384},{640,512},{768,640},... | collective-permute-start | bytes 1572872 | tf_op jit(solution)/shard_map/ppermute | solution.py:310
  68.9 1.9 %collective-permute-start.2 = (bf16[2048,128]{1,0:T(8,128)(2,1)S(1)}, bf16[2048,128]{1,0:T(8,128)(2,1)S(1)}, u32[]{:S(2)}, u32[]{:S(2)}) collective-permute-start(bf16[2048,128]{1,0:T(8,128)(2,1)S(1)} %ahead.3), channel_id=1, source_target_pairs={{0,128},{128,256},{256,384},{384,512},{512,640},{640,768},{768,896... | collective-permute-start | bytes 1572872 | tf_op jit(solution)/shard_map/ppermute | solution.py:307
  70.8 1.3 %returns.1 = (f32[512,512]{1,0:T(8,128)S(1)}, bf16[512,512]{1,0:T(8,128)(2,1)S(1)}) custom-call(s32[1]{0:T(128)} %bitcast.m_ref, bf16[256,1024]{1,0:T(8,128)(2,1)S(1)} %get-tuple-element.38.hid_ref, bf16[256,1024]{1,0:T(8,128)(2,1)S(1)} %get-tuple-element.32.pg_ref, bf16[1024,1024]{1,0:T(8,128)(2,1)S(1)} %get-tuple-element.27.up_ref, ...), custom_call_target="tpu_custom_call" | custom-call | tf_op jit(solution)/shard_map/returns/pallas_call | solution.py:219
  72.1 1.9 %collective-permute-start.5 = (bf16[512,512]{1,0:T(8,128)(2,1)S(1)}, bf16[512,512]{1,0:T(8,128)(2,1)S(1)}, u32[]{:S(2)}, u32[]{:S(2)}) collective-permute-start(bf16[512,512]{1,0:T(8,128)(2,1)S(1)} %get-tuple-element.40), channel_id=1, source_target_pairs={{0,1},{1,0},{2,3},{3,2},{4,5},{5,4},{6,7},{7,6},{8,9},{9,8},{10,11... | collective-permute-start | bytes 1572872 | tf_op jit(solution)/shard_map/ppermute | solution.py:345
  74.0 5.8 %collective-permute-done.4.got_ref = bf16[2048,128]{1,0:T(8,128)(2,1)S(1)} collective-permute-done((bf16[2048,128]{1,0:T(8,128)(2,1)S(1)}, bf16[2048,128]{1,0:T(8,128)(2,1)S(1)}, u32[]{:S(2)}, u32[]{:S(2)}) %collective-permute-start.4) | collective-permute-done | bytes 524320 | tf_op jit(solution)/shard_map/ppermute | solution.py:310
  79.9 0.1 behind.4.also_ref
  80.0 5.6 %collective-permute-start.7 = (bf16[2048,128]{1,0:T(8,128)(2,1)S(1)}, bf16[2048,128]{1,0:T(8,128)(2,1)}, u32[]{:S(2)}, u32[]{:S(2)}) collective-permute-start(bf16[2048,128]{1,0:T(8,128)(2,1)S(1)} %behind.4.also_ref), channel_id=1, source_target_pairs={{0,896},{128,0},{256,128},{384,256},{512,384},{640,512},{768,640},... | collective-permute-start | bytes 1572872 | tf_op jit(solution)/shard_map/ppermute | solution.py:310
  85.6 0.1 ahead.4.after_ref
  85.8 1.9 %collective-permute-start.9 = (bf16[2048,128]{1,0:T(8,128)(2,1)S(1)}, bf16[2048,128]{1,0:T(8,128)(2,1)}, u32[]{:S(2)}, u32[]{:S(2)}) collective-permute-start(bf16[2048,128]{1,0:T(8,128)(2,1)S(1)} %ahead.4.after_ref), channel_id=1, source_target_pairs={{0,128},{128,256},{256,384},{384,512},{512,640},{640,768},{768,896... | collective-permute-start | bytes 1572872 | tf_op jit(solution)/shard_map/ppermute | solution.py:307
  87.7 1.3 %add.1 = bf16[512,512]{1,0:T(8,128)(2,1)} custom-call(bf16[2048,128]{1,0:T(8,128)(2,1)S(1)} %ahead.4.after_ref, bf16[2048,128]{1,0:T(8,128)(2,1)S(1)} %behind.4.also_ref, f32[512,512]{1,0:T(8,128)S(1)} %get-tuple-element.39.keep_ref, bf16[512,512]{1,0:T(8,128)(2,1)S(1)} %collective-permute-done.5.got_ref), custom_call_target="tpu_custom_call" | custom-call | tf_op jit(solution)/shard_map/add/pallas_call | solution.py:219
  88.9 5.2 %all-to-all-start.1 = ((bf16[64,8,512]{2,1,0:T(8,128)(2,1)}), bf16[64,8,512]{2,1,0:T(8,128)(2,1)S(1)}, u32[]{:S(2)}, u32[]{:S(2)}) async-start(bf16[64,8,512]{2,1,0:T(8,128)(2,1)} %bitcast.7), calls=%async_computation.1 | async-start | bytes 1048576 | tf_op jit(solution)/shard_map/all_to_all | solution.py:332
  94.2 1.6 %collective-permute-done.7.got_ref = bf16[2048,128]{1,0:T(8,128)(2,1)} collective-permute-done((bf16[2048,128]{1,0:T(8,128)(2,1)S(1)}, bf16[2048,128]{1,0:T(8,128)(2,1)}, u32[]{:S(2)}, u32[]{:S(2)}) %collective-permute-start.7) | collective-permute-done | bytes 524320 | tf_op jit(solution)/shard_map/ppermute | solution.py:310
  95.8 2.0 %behind.5 = bf16[2048,128]{1,0:T(8,128)(2,1)} custom-call(bf16[2048,128]{1,0:T(8,128)(2,1)} %collective-permute-done.7.got_ref, bf16[2048,128]{1,0:T(8,128)(2,1)S(1)} %get-tuple-element.43.part_ref), custom_call_target="tpu_custom_call" | custom-call | flops 2000000000 | bytes 6000000 | tf_op jit(solution)/shard_map/behind/pallas_call | solution.py:219
  97.7 5.7 %collective-permute-start.8 = (bf16[2048,128]{1,0:T(8,128)(2,1)}, bf16[2048,128]{1,0:T(8,128)(2,1)S(1)}, u32[]{:S(2)}, u32[]{:S(2)}) collective-permute-start(bf16[2048,128]{1,0:T(8,128)(2,1)} %behind.5), channel_id=1, source_target_pairs={{0,896},{128,0},{256,128},{384,256},{512,384},{640,512},{768,640},... | collective-permute-start | bytes 1572872 | tf_op jit(solution)/shard_map/ppermute | solution.py:310
  103.5 2.0 %ahead.5 = bf16[2048,128]{1,0:T(8,128)(2,1)} custom-call(bf16[2048,128]{1,0:T(8,128)(2,1)} %collective-permute-done.9.got_ref, bf16[2048,128]{1,0:T(8,128)(2,1)S(1)} %get-tuple-element.44.part_ref), custom_call_target="tpu_custom_call" | custom-call | flops 4000000000 | bytes 12000000 | tf_op jit(solution)/shard_map/ahead/pallas_call | solution.py:219
  105.5 1.9 %collective-permute-start.10 = (bf16[2048,128]{1,0:T(8,128)(2,1)}, bf16[2048,128]{1,0:T(8,128)(2,1)S(1)}, u32[]{:S(2)}, u32[]{:S(2)}) collective-permute-start(bf16[2048,128]{1,0:T(8,128)(2,1)} %ahead.5), channel_id=1, source_target_pairs={{0,128},{128,256},{256,384},{384,512},{512,640},{640,768},{768,896... | collective-permute-start | bytes 1572872 | tf_op jit(solution)/shard_map/ppermute | solution.py:307
  107.4 4.9 %all-to-all-done.1 = bf16[64,8,512]{2,1,0:T(8,128)(2,1)S(1)} async-done(((bf16[64,8,512]{2,1,0:T(8,128)(2,1)}), bf16[64,8,512]{2,1,0:T(8,128)(2,1)S(1)}, u32[]{:S(2)}, u32[]{:S(2)}) %all-to-all-start.1) | async-done | bytes 524320 | tf_op jit(solution)/shard_map/all_to_all | solution.py:332
  112.3 0.4 home.1.mine_ref
  112.7 1.9 %collective-permute-start.6 = (bf16[256,512]{1,0:T(8,128)(2,1)S(1)}, bf16[256,512]{1,0:T(8,128)(2,1)S(1)}, u32[]{:S(2)}, u32[]{:S(2)}) collective-permute-start(bf16[256,512]{1,0:T(8,128)(2,1)S(1)} %home.1.mine_ref), channel_id=1, source_target_pairs={{0,1},{1,0},{2,3},{3,2},{4,5},{5,4},{6,7},{7,6},{8,9},{9,8},{10,11... | collective-permute-start | bytes 786440 | tf_op jit(solution)/shard_map/ppermute | solution.py:353
  114.6 1.5 %collective-permute-done.6.other_ref = bf16[256,512]{1,0:T(8,128)(2,1)S(1)} collective-permute-done((bf16[256,512]{1,0:T(8,128)(2,1)S(1)}, bf16[256,512]{1,0:T(8,128)(2,1)S(1)}, u32[]{:S(2)}, u32[]{:S(2)}) %collective-permute-start.6) | collective-permute-done | bytes 262176 | tf_op jit(solution)/shard_map/ppermute | solution.py:353
  116.1 1.0 final.1
  117.2 3.1 %collective-permute-done.10.right_ref = bf16[2048,128]{1,0:T(8,128)(2,1)S(1)} collective-permute-done((bf16[2048,128]{1,0:T(8,128)(2,1)}, bf16[2048,128]{1,0:T(8,128)(2,1)S(1)}, u32[]{:S(2)}, u32[]{:S(2)}) %collective-permute-start.10) | collective-permute-done | bytes 524320 | tf_op jit(solution)/shard_map/ppermute | solution.py:307
  120.2 1.1 last.1
  (14 shorter events, 0.2 us)
Async XLA Ops:
  44.1 4.2 %collective-permute-start = (bf16[512,512]{1,0:T(8,128)(2,1)S(1)}, bf16[512,512]{1,0:T(8,128)(2,1)S(1)}, u32[]{:S(2)}, u32[]{:S(2)}) collective-permute-start(bf16[512,512]{1,0:T(8,128)(2,1)S(1)} %bitcast.11), channel_id=1, source_target_pairs={{0,1},{1,0},{2,3},{3,2},{4,5},{5,4},{6,7},{7,6},{8,9},{9,8},{10,11... | collective-permute-start | bytes 1572872 | tf_op jit(solution)/shard_map/ppermute | solution.py:337
  50.8 12.4 %collective-permute-start.3 = (bf16[1024,128]{1,0:T(8,128)(2,1)S(1)}, bf16[1024,128]{1,0:T(8,128)(2,1)S(1)}, u32[]{:S(2)}, u32[]{:S(2)}) collective-permute-start(bf16[1024,128]{1,0:T(8,128)(2,1)S(1)} %get-tuple-element.35), channel_id=1, source_target_pairs={{0,896},{128,0},{256,128},{384,256},{512,384},{640,512},{768,640},... | collective-permute-start | bytes 786440 | tf_op jit(solution)/shard_map/ppermute | solution.py:295
  56.9 11.9 %collective-permute-start.1 = (bf16[1024,128]{1,0:T(8,128)(2,1)S(1)}, bf16[1024,128]{1,0:T(8,128)(2,1)S(1)}, u32[]{:S(2)}, u32[]{:S(2)}) collective-permute-start(bf16[1024,128]{1,0:T(8,128)(2,1)S(1)} %get-tuple-element.29), channel_id=1, source_target_pairs={{0,128},{128,256},{256,384},{384,512},{512,640},{640,768},{768,896... | collective-permute-start | bytes 786440 | tf_op jit(solution)/shard_map/ppermute | solution.py:294
  63.2 16.6 %collective-permute-start.4 = (bf16[2048,128]{1,0:T(8,128)(2,1)S(1)}, bf16[2048,128]{1,0:T(8,128)(2,1)S(1)}, u32[]{:S(2)}, u32[]{:S(2)}) collective-permute-start(bf16[2048,128]{1,0:T(8,128)(2,1)S(1)} %behind.3), channel_id=1, source_target_pairs={{0,896},{128,0},{256,128},{384,256},{512,384},{640,512},{768,640},... | collective-permute-start | bytes 1572872 | tf_op jit(solution)/shard_map/ppermute | solution.py:310
  68.9 16.7 %collective-permute-start.2 = (bf16[2048,128]{1,0:T(8,128)(2,1)S(1)}, bf16[2048,128]{1,0:T(8,128)(2,1)S(1)}, u32[]{:S(2)}, u32[]{:S(2)}) collective-permute-start(bf16[2048,128]{1,0:T(8,128)(2,1)S(1)} %ahead.3), channel_id=1, source_target_pairs={{0,128},{128,256},{256,384},{384,512},{512,640},{640,768},{768,896... | collective-permute-start | bytes 1572872 | tf_op jit(solution)/shard_map/ppermute | solution.py:307
  72.1 15.6 %collective-permute-start.5 = (bf16[512,512]{1,0:T(8,128)(2,1)S(1)}, bf16[512,512]{1,0:T(8,128)(2,1)S(1)}, u32[]{:S(2)}, u32[]{:S(2)}) collective-permute-start(bf16[512,512]{1,0:T(8,128)(2,1)S(1)} %get-tuple-element.40), channel_id=1, source_target_pairs={{0,1},{1,0},{2,3},{3,2},{4,5},{5,4},{6,7},{7,6},{8,9},{9,8},{10,11... | collective-permute-start | bytes 1572872 | tf_op jit(solution)/shard_map/ppermute | solution.py:345
  80.0 15.8 %collective-permute-start.7 = (bf16[2048,128]{1,0:T(8,128)(2,1)S(1)}, bf16[2048,128]{1,0:T(8,128)(2,1)}, u32[]{:S(2)}, u32[]{:S(2)}) collective-permute-start(bf16[2048,128]{1,0:T(8,128)(2,1)S(1)} %behind.4.also_ref), channel_id=1, source_target_pairs={{0,896},{128,0},{256,128},{384,256},{512,384},{640,512},{768,640},... | collective-permute-start | bytes 1572872 | tf_op jit(solution)/shard_map/ppermute | solution.py:310
  85.8 17.7 %collective-permute-start.9 = (bf16[2048,128]{1,0:T(8,128)(2,1)S(1)}, bf16[2048,128]{1,0:T(8,128)(2,1)}, u32[]{:S(2)}, u32[]{:S(2)}) collective-permute-start(bf16[2048,128]{1,0:T(8,128)(2,1)S(1)} %ahead.4.after_ref), channel_id=1, source_target_pairs={{0,128},{128,256},{256,384},{384,512},{512,640},{640,768},{768,896... | collective-permute-start | bytes 1572872 | tf_op jit(solution)/shard_map/ppermute | solution.py:307
  88.9 23.3 %all-to-all-start.1 = ((bf16[64,8,512]{2,1,0:T(8,128)(2,1)}), bf16[64,8,512]{2,1,0:T(8,128)(2,1)S(1)}, u32[]{:S(2)}, u32[]{:S(2)}) async-start(bf16[64,8,512]{2,1,0:T(8,128)(2,1)} %bitcast.7), calls=%async_computation.1 | async-start | bytes 1048576 | tf_op jit(solution)/shard_map/all_to_all | solution.py:332
  97.7 19.5 %collective-permute-start.8 = (bf16[2048,128]{1,0:T(8,128)(2,1)}, bf16[2048,128]{1,0:T(8,128)(2,1)S(1)}, u32[]{:S(2)}, u32[]{:S(2)}) collective-permute-start(bf16[2048,128]{1,0:T(8,128)(2,1)} %behind.5), channel_id=1, source_target_pairs={{0,896},{128,0},{256,128},{384,256},{512,384},{640,512},{768,640},... | collective-permute-start | bytes 1572872 | tf_op jit(solution)/shard_map/ppermute | solution.py:310
  103.4 8.9 %copy-start.2 = (s32[32,1]{0,1:T(1,128)S(1)}, s32[32,1]{0,1:T(1,128)}, u32[]{:S(2)}) copy-start(s32[32,1]{0,1:T(1,128)} %param.6) | copy-start | bytes 388
  103.4 12.7 %copy-start = (f32[128,1024]{1,0:T(8,128)S(1)}, f32[128,1024]{1,0:T(8,128)}, u32[]{:S(2)}) copy-start(f32[128,1024]{1,0:T(8,128)} %tok_ref.3) | copy-start | bytes 1572868
  103.4 12.7 %copy-start.1 = (f32[128,1024]{1,0:T(8,128)S(1)}, f32[128,1024]{1,0:T(8,128)}, u32[]{:S(2)}) copy-start(f32[128,1024]{1,0:T(8,128)} %up_ref.3) | copy-start | bytes 1572868
  105.5 14.8 %collective-permute-start.10 = (bf16[2048,128]{1,0:T(8,128)(2,1)}, bf16[2048,128]{1,0:T(8,128)(2,1)S(1)}, u32[]{:S(2)}, u32[]{:S(2)}) collective-permute-start(bf16[2048,128]{1,0:T(8,128)(2,1)} %ahead.5), channel_id=1, source_target_pairs={{0,128},{128,256},{256,384},{384,512},{512,640},{640,768},{768,896... | collective-permute-start | bytes 1572872 | tf_op jit(solution)/shard_map/ppermute | solution.py:307
  112.7 3.4 %collective-permute-start.6 = (bf16[256,512]{1,0:T(8,128)(2,1)S(1)}, bf16[256,512]{1,0:T(8,128)(2,1)S(1)}, u32[]{:S(2)}, u32[]{:S(2)}) collective-permute-start(bf16[256,512]{1,0:T(8,128)(2,1)S(1)} %home.1.mine_ref), channel_id=1, source_target_pairs={{0,1},{1,0},{2,3},{3,2},{4,5},{5,4},{6,7},{7,6},{8,9},{9,8},{10,11... | collective-permute-start | bytes 786440 | tf_op jit(solution)/shard_map/ppermute | solution.py:353

commit v5 on v4

--- a/solution.py
+++ b/solution.py
@@ -195,10 +195,6 @@
 
 
 PARAMS = pltpu.CompilerParams(vmem_limit_bytes=16 * 2**20)
-def long(us):
-    return pl.CostEstimate(flops=us * 1_000_000_000, bytes_accessed=us * 3_000_000, transcendentals=0)
-
-
 ONCHIP = pl.BlockSpec(memory_space=pltpu.VMEM)
 
 
@@ -210,7 +206,7 @@
     return pltpu.with_memory_space_constraint(array, pltpu.HBM)
 
 
-def call(kernel, outs, scalars, name, after=0, cost=None):
+def call(kernel, outs, scalars, name, after=0):
     one = not isinstance(outs, tuple)
     unread = [pl.BlockSpec(memory_space=pl.ANY)] * after
 
@@ -222,7 +218,6 @@
             in_specs=[pl.BlockSpec(memory_space=pltpu.SMEM)] * scalars + unread + [ONCHIP] * arrays,
             out_specs=ONCHIP if one else (ONCHIP,) * len(outs),
             compiler_params=PARAMS,
-            cost_estimate=cost,
             name=name,
         )(*args)
 
@@ -302,15 +297,15 @@
     sent = []
     for hop in range(half - 1, 0, -1):
         whole = hop < half - 1
-        step = call(functools.partial(hop_kernel, None if whole else False), size, 0, "ahead", 0, long(4) if hop == 1 else None)
+        step = call(functools.partial(hop_kernel, None if whole else False), size, 0, "ahead")
         sent.append(step(onchip(right), onchip(parts[hop])))
         right = lax.ppermute(sent[-1], "dp", ahead)
-        step = call(functools.partial(hop_kernel, None if whole else True), size, 0, "behind", 0, long(2) if hop == 1 else None)
+        step = call(functools.partial(hop_kernel, None if whole else True), size, 0, "behind")
         sent.append(step(onchip(left), onchip(parts[groups - hop])))
         left = lax.ppermute(sent[-1], "dp", behind)
     def finish(after):
         outs = (shape((share, hidden_cols), F32), shape((hidden_cols, share), F32))
-        return call(last_kernel, outs, 0, "last", 1)(offchip(after), onchip(left), onchip(right), onchip(parts[0]))
+        return call(last_kernel, outs, 0, "last", 1)(offchip(after), onchip(left), onchip(right), offchip(parts[0]))
 
     return finish, hidden, pre_grad, sent
 
@@ -344,7 +339,7 @@
     )(m, onchip(hidden), onchip(pre_grad), onchip(up_matrix), onchip(down_matrix))
     got = lax.ppermute(send, "mp", swap)
     added = call(functools.partial(add_kernel, block), pltpu.VMEM((rows, half_cols), BF16), 0, "add", 2)(
-        sent[2], sent[3], onchip(keep), onchip(got)
+        sent[0], sent[1], onchip(keep), onchip(got)
     )
     back = exchange(added)
     home = call(functools.partial(home_kernel, block), pltpu.VMEM((2 * tok_rows, half_cols), BF16), 0, "home")(

time: 122 us -> 124 us (1.016)
  waiting for transfers between devices: 19.9 us -> 21.2 us
    ppermute x3, waiting for transfers between devices: 7.4 us -> 12.4 us  [weight_grads(): left = lax.ppermute(sent[-1], 'dp', behind)]
    all_to_all x1, waiting for transfers between devices: 4.88 us -> 0.01 us  [exchange(): lax.all_to_all(shaped, 'expert', split_axis=0, concat_axis=0, tiled=True)]
    ppermute x3, waiting for transfers between devices: 3.09 us -> 7.34 us  [weight_grads(): right = lax.ppermute(sent[-1], 'dp', ahead)]
    ppermute x1, waiting for transfers between devices: 3.05 us -> 0.01 us  [weight_grads(): left = lax.ppermute(far_down, 'dp', behind)]
  transfers between devices with their start and end apart: 12 -> 12, of which waited for: 6 -> 6; matrix products, arithmetic and copies ran while one was open for 0% -> 0% of each run, Pallas kernels for 10% -> 8%
where the time goes in v5:
time: 124 us; the launch traced here: 123 us
  blocking collectives  41.9 us (34%)
  starting transfers between devices  41.7 us (34%)
  waiting for transfers between devices  21.2 us (17%)
  Pallas kernels  16.5 us (13%)
    all_to_all x1, blocking collectives, exchange(): lax.all_to_all(shaped, 'expert', split_axis=0, concat_axis=0, tiled=True)  41.9 us
    ppermute x3, starting transfers between devices, weight_grads(): left = lax.ppermute(sent[-1], 'dp', behind)  16.5 us
    ppermute x3, waiting for transfers between devices, weight_grads(): left = lax.ppermute(sent[-1], 'dp', behind)  12.4 us
    pallas_call x12, Pallas kernels, run(): pl.pallas_call(kernel, out_shape=outs, in_specs=[pl.BlockSpec(memory_spac...  10.2 us
    ppermute x3, waiting for transfers between devices, weight_grads(): right = lax.ppermute(sent[-1], 'dp', ahead)  7.34 us
    ppermute x1, starting transfers between devices, weight_grads(): left = lax.ppermute(far_down, 'dp', behind)  6.17 us
    ppermute x3, starting transfers between devices, weight_grads(): right = lax.ppermute(sent[-1], 'dp', ahead)  5.89 us
    all_to_all x1, starting transfers between devices, exchange(): lax.all_to_all(shaped, 'expert', split_axis=0, concat_axis=0, tiled=True)  5.21 us
  transfers between devices with their start and end apart: 12, of which 6 were waited for; matrix products, arithmetic and copies ran while one was open for 0% of the time, Pallas kernels for 8%

profile of v5, /device:TPU:4, one launch (start us, length us, event | category | flops | bytes accessed | tf_op | source)
XLA Modules:
  0.0 123.2 jit_solution(5562982001269064920)
XLA Ops:
  0.6 1.6 %slots.1 = bf16[512,512]{1,0:T(8,128)(2,1)S(1)} custom-call(s32[1]{0:T(128)} %bitcast.m_ref, s32[1,32]{1,0:T(1,128)} %bitcast.15, f32[128,1024]{1,0:T(8,128)} %tok_ref.3, f32[128,1024]{1,0:T(8,128)} %up_ref.3), custom_call_target="tpu_custom_call" | custom-call | tf_op jit(solution)/shard_map/slots/pallas_call | solution.py:234
  2.2 41.9 %all_to_all.10 = bf16[64,8,512]{2,1,0:T(8,128)(2,1)S(1)} all-to-all(bf16[64,8,512]{2,1,0:T(8,128)(2,1)S(1)} %bitcast.14), channel_id=1, replica_groups=mesh['dp'=8,'expert'=64,'mp'=2] {'expert'}, dimensions={0} | all-to-all | bytes 1048576 | tf_op jit(solution)/shard_map/all_to_all | solution.py:327
  44.1 1.9 %collective-permute-start = (bf16[512,512]{1,0:T(8,128)(2,1)S(1)}, bf16[512,512]{1,0:T(8,128)(2,1)S(1)}, u32[]{:S(2)}, u32[]{:S(2)}) collective-permute-start(bf16[512,512]{1,0:T(8,128)(2,1)S(1)} %bitcast.11), channel_id=1, source_target_pairs={{0,1},{1,0},{2,3},{3,2},{4,5},{5,4},{6,7},{7,6},{8,9},{9,8},{10,11... | collective-permute-start | bytes 1572872 | tf_op jit(solution)/shard_map/ppermute | solution.py:332
  46.0 2.3 %front.1 = (bf16[512,512]{1,0:T(8,128)(2,1)S(1)}, bf16[1024,1024]{1,0:T(8,128)(2,1)S(1)}, bf16[1024,1024]{1,0:T(8,128)(2,1)S(1)}) custom-call(bf16[512,512]{1,0:T(8,128)(2,1)S(1)} %bitcast.12, bf16[1024,1024]{1,0:T(8,128)(2,1)} %bitcast.17, bf16[1024,1024]{1,0:T(8,128)(2,1)} %bitcast.18), custom_call_target="tpu_custom_call" | custom-call | tf_op jit(solution)/shard_map/front/pallas_call | solution.py:250
  48.3 2.5 %hidden.1 = (bf16[1024,128]{1,0:T(8,128)(2,1)S(1)}, bf16[1024,128]{1,0:T(8,128)(2,1)S(1)}, bf16[256,1024]{1,0:T(8,128)(2,1)S(1)}, bf16[256,1024]{1,0:T(8,128)(2,...) custom-call(s32[1]{0:T(128)} %bitcast.m_ref, s32[1]{0:T(128)} %bitcast.2.group_ref, ...), custom_call_target="tpu_custom_call" | custom-call | tf_op jit(solution)/shard_map/hidden/pallas_call | solution.py:271
  50.8 6.2 %collective-permute-start.2 = (bf16[1024,128]{1,0:T(8,128)(2,1)S(1)}, bf16[1024,128]{1,0:T(8,128)(2,1)S(1)}, u32[]{:S(2)}, u32[]{:S(2)}) collective-permute-start(bf16[1024,128]{1,0:T(8,128)(2,1)S(1)} %get-tuple-element.34), channel_id=1, source_target_pairs={{0,896},{128,0},{256,128},{384,256},{512,384},{640,512},{768,640},... | collective-permute-start | bytes 786440 | tf_op jit(solution)/shard_map/ppermute | solution.py:290
  56.9 1.9 %collective-permute-start.1 = (bf16[1024,128]{1,0:T(8,128)(2,1)S(1)}, bf16[1024,128]{1,0:T(8,128)(2,1)S(1)}, u32[]{:S(2)}, u32[]{:S(2)}) collective-permute-start(bf16[1024,128]{1,0:T(8,128)(2,1)S(1)} %get-tuple-element.29), channel_id=1, source_target_pairs={{0,128},{128,256},{256,384},{384,512},{512,640},{640,768},{768,896... | collective-permute-start | bytes 786440 | tf_op jit(solution)/shard_map/ppermute | solution.py:289
  58.9 1.3 %returns.1 = (f32[512,512]{1,0:T(8,128)S(1)}, bf16[512,512]{1,0:T(8,128)(2,1)S(1)}) custom-call(s32[1]{0:T(128)} %bitcast.m_ref, bf16[256,1024]{1,0:T(8,128)(2,1)S(1)} %get-tuple-element.36.hid_ref, bf16[256,1024]{1,0:T(8,128)(2,1)S(1)} %get-tuple-element.32.pg_ref, bf16[1024,1024]{1,0:T(8,128)(2,1)S(1)} %get-tuple-element.27.up_ref, ...), custom_call_target="tpu_custom_call" | custom-call | tf_op jit(solution)/shard_map/returns/pallas_call | solution.py:215
  60.1 2.1 %collective-permute-start.3 = (bf16[512,512]{1,0:T(8,128)(2,1)S(1)}, bf16[512,512]{1,0:T(8,128)(2,1)S(1)}, u32[]{:S(2)}, u32[]{:S(2)}) collective-permute-start(bf16[512,512]{1,0:T(8,128)(2,1)S(1)} %get-tuple-element.38), channel_id=1, source_target_pairs={{0,1},{1,0},{2,3},{3,2},{4,5},{5,4},{6,7},{7,6},{8,9},{9,8},{10,11... | collective-permute-start | bytes 1572872 | tf_op jit(solution)/shard_map/ppermute | solution.py:340
  62.3 1.2 shares.1
  63.6 5.2 %collective-permute-start.5 = (bf16[2048,128]{1,0:T(8,128)(2,1)S(1)}, bf16[2048,128]{1,0:T(8,128)(2,1)}, u32[]{:S(2)}, u32[]{:S(2)}) collective-permute-start(bf16[2048,128]{1,0:T(8,128)(2,1)S(1)} %behind.3.also_ref), channel_id=1, source_target_pairs={{0,896},{128,0},{256,128},{384,256},{512,384},{640,512},{768,640},... | collective-permute-start | bytes 1572872 | tf_op jit(solution)/shard_map/ppermute | solution.py:305
  68.9 1.9 %collective-permute-start.8 = (bf16[2048,128]{1,0:T(8,128)(2,1)S(1)}, bf16[2048,128]{1,0:T(8,128)(2,1)}, u32[]{:S(2)}, u32[]{:S(2)}) collective-permute-start(bf16[2048,128]{1,0:T(8,128)(2,1)S(1)} %ahead.3.after_ref), channel_id=1, source_target_pairs={{0,128},{128,256},{256,384},{384,512},{512,640},{640,768},{768,896... | collective-permute-start | bytes 1572872 | tf_op jit(solution)/shard_map/ppermute | solution.py:302
  70.9 1.3 %add.1 = bf16[512,512]{1,0:T(8,128)(2,1)} custom-call(bf16[2048,128]{1,0:T(8,128)(2,1)S(1)} %ahead.3.after_ref, bf16[2048,128]{1,0:T(8,128)(2,1)S(1)} %behind.3.also_ref, f32[512,512]{1,0:T(8,128)S(1)} %get-tuple-element.37.keep_ref, bf16[512,512]{1,0:T(8,128)(2,1)S(1)} %collective-permute-done.3.got_ref), custom_call_target="tpu_custom_call" | custom-call | tf_op jit(solution)/shard_map/add/pallas_call | solution.py:215
  72.2 5.2 %all-to-all-start.1 = ((bf16[64,8,512]{2,1,0:T(8,128)(2,1)}), bf16[64,8,512]{2,1,0:T(8,128)(2,1)S(1)}, u32[]{:S(2)}, u32[]{:S(2)}) async-start(bf16[64,8,512]{2,1,0:T(8,128)(2,1)} %bitcast.7), calls=%async_computation.1 | async-start | bytes 1048576 | tf_op jit(solution)/shard_map/all_to_all | solution.py:327
  77.4 3.0 %collective-permute-done.5.got_ref = bf16[2048,128]{1,0:T(8,128)(2,1)} collective-permute-done((bf16[2048,128]{1,0:T(8,128)(2,1)S(1)}, bf16[2048,128]{1,0:T(8,128)(2,1)}, u32[]{:S(2)}, u32[]{:S(2)}) %collective-permute-start.5) | collective-permute-done | bytes 524320 | tf_op jit(solution)/shard_map/ppermute | solution.py:305
  80.4 1.0 copy-done.3
  81.4 1.2 behind.4
  82.6 5.7 %collective-permute-start.6 = (bf16[2048,128]{1,0:T(8,128)(2,1)S(1)}, bf16[2048,128]{1,0:T(8,128)(2,1)S(1)}, u32[]{:S(2)}, u32[]{:S(2)}) collective-permute-start(bf16[2048,128]{1,0:T(8,128)(2,1)S(1)} %behind.4), channel_id=1, source_target_pairs={{0,896},{128,0},{256,128},{384,256},{512,384},{640,512},{768,640},... | collective-permute-start | bytes 1572872 | tf_op jit(solution)/shard_map/ppermute | solution.py:305
  88.3 1.2 ahead.4
  89.5 2.1 %collective-permute-start.9 = (bf16[2048,128]{1,0:T(8,128)(2,1)S(1)}, bf16[2048,128]{1,0:T(8,128)(2,1)S(1)}, u32[]{:S(2)}, u32[]{:S(2)}) collective-permute-start(bf16[2048,128]{1,0:T(8,128)(2,1)S(1)} %ahead.4), channel_id=1, source_target_pairs={{0,128},{128,256},{256,384},{384,512},{512,640},{640,768},{768,896... | collective-permute-start | bytes 1572872 | tf_op jit(solution)/shard_map/ppermute | solution.py:302
  91.6 7.5 %collective-permute-done.6.got_ref = bf16[2048,128]{1,0:T(8,128)(2,1)S(1)} collective-permute-done((bf16[2048,128]{1,0:T(8,128)(2,1)S(1)}, bf16[2048,128]{1,0:T(8,128)(2,1)S(1)}, u32[]{:S(2)}, u32[]{:S(2)}) %collective-permute-start.6) | collective-permute-done | bytes 524320 | tf_op jit(solution)/shard_map/ppermute | solution.py:305
  99.0 0.1 behind.5
  99.2 5.6 %collective-permute-start.7 = (bf16[2048,128]{1,0:T(8,128)(2,1)S(1)}, bf16[2048,128]{1,0:T(8,128)(2,1)}, u32[]{:S(2)}, u32[]{:S(2)}) collective-permute-start(bf16[2048,128]{1,0:T(8,128)(2,1)S(1)} %behind.5), channel_id=1, source_target_pairs={{0,896},{128,0},{256,128},{384,256},{512,384},{640,512},{768,640},... | collective-permute-start | bytes 1572872 | tf_op jit(solution)/shard_map/ppermute | solution.py:305
  104.8 0.9 collective-permute-done.9.got_ref
  105.8 1.9 %collective-permute-start.10 = (bf16[2048,128]{1,0:T(8,128)(2,1)S(1)}, bf16[2048,128]{1,0:T(8,128)(2,1)S(1)}, u32[]{:S(2)}, u32[]{:S(2)}) collective-permute-start(bf16[2048,128]{1,0:T(8,128)(2,1)S(1)} %ahead.5), channel_id=1, source_target_pairs={{0,128},{128,256},{256,384},{384,512},{512,640},{640,768},{768,896... | collective-permute-start | bytes 1572872 | tf_op jit(solution)/shard_map/ppermute | solution.py:302
  107.8 0.4 home.1.mine_ref
  108.2 1.9 %collective-permute-start.4 = (bf16[256,512]{1,0:T(8,128)(2,1)S(1)}, bf16[256,512]{1,0:T(8,128)(2,1)S(1)}, u32[]{:S(2)}, u32[]{:S(2)}) collective-permute-start(bf16[256,512]{1,0:T(8,128)(2,1)S(1)} %home.1.mine_ref), channel_id=1, source_target_pairs={{0,1},{1,0},{2,3},{3,2},{4,5},{5,4},{6,7},{7,6},{8,9},{9,8},{10,11... | collective-permute-start | bytes 786440 | tf_op jit(solution)/shard_map/ppermute | solution.py:348
  110.1 1.5 %collective-permute-done.4.other_ref = bf16[256,512]{1,0:T(8,128)(2,1)S(1)} collective-permute-done((bf16[256,512]{1,0:T(8,128)(2,1)S(1)}, bf16[256,512]{1,0:T(8,128)(2,1)S(1)}, u32[]{:S(2)}, u32[]{:S(2)}) %collective-permute-start.4) | collective-permute-done | bytes 262176 | tf_op jit(solution)/shard_map/ppermute | solution.py:348
  111.6 1.0 final.1
  112.7 1.9 %collective-permute-done.7.left_ref = bf16[2048,128]{1,0:T(8,128)(2,1)} collective-permute-done((bf16[2048,128]{1,0:T(8,128)(2,1)S(1)}, bf16[2048,128]{1,0:T(8,128)(2,1)}, u32[]{:S(2)}, u32[]{:S(2)}) %collective-permute-start.7) | collective-permute-done | bytes 524320 | tf_op jit(solution)/shard_map/ppermute | solution.py:305
  114.6 6.4 %collective-permute-done.10.right_ref = bf16[2048,128]{1,0:T(8,128)(2,1)S(1)} collective-permute-done((bf16[2048,128]{1,0:T(8,128)(2,1)S(1)}, bf16[2048,128]{1,0:T(8,128)(2,1)S(1)}, u32[]{:S(2)}, u32[]{:S(2)}) %collective-permute-start.10) | collective-permute-done | bytes 524320 | tf_op jit(solution)/shard_map/ppermute | solution.py:302
  121.0 2.3 %last.1 = (f32[128,1024]{1,0:T(8,128)}, f32[1024,128]{1,0:T(8,128)}) custom-call(f32[128,1024]{1,0:T(8,128)} %get-tuple-element.23.after_ref, bf16[2048,128]{1,0:T(8,128)(2,1)} %collective-permute-done.7.left_ref, bf16[2048,128]{1,0:T(8,128)(2,1)S(1)} %collective-permute-done.10.right_ref, bf16[2048,128]{1,0:T(8,128)(2,1)} %copy-done.4), custom_call_target="tpu_custom_call" | custom-call | tf_op jit(solution)/shard_map/last/pallas_call | solution.py:215
  (20 shorter events, 0.3 us)
Async XLA Ops:
  44.1 4.2 %collective-permute-start = (bf16[512,512]{1,0:T(8,128)(2,1)S(1)}, bf16[512,512]{1,0:T(8,128)(2,1)S(1)}, u32[]{:S(2)}, u32[]{:S(2)}) collective-permute-start(bf16[512,512]{1,0:T(8,128)(2,1)S(1)} %bitcast.11), channel_id=1, source_target_pairs={{0,1},{1,0},{2,3},{3,2},{4,5},{5,4},{6,7},{7,6},{8,9},{9,8},{10,11... | collective-permute-start | bytes 1572872 | tf_op jit(solution)/shard_map/ppermute | solution.py:332
  50.8 12.8 %collective-permute-start.2 = (bf16[1024,128]{1,0:T(8,128)(2,1)S(1)}, bf16[1024,128]{1,0:T(8,128)(2,1)S(1)}, u32[]{:S(2)}, u32[]{:S(2)}) collective-permute-start(bf16[1024,128]{1,0:T(8,128)(2,1)S(1)} %get-tuple-element.34), channel_id=1, source_target_pairs={{0,896},{128,0},{256,128},{384,256},{512,384},{640,512},{768,640},... | collective-permute-start | bytes 786440 | tf_op jit(solution)/shard_map/ppermute | solution.py:290
  56.9 11.9 %collective-permute-start.1 = (bf16[1024,128]{1,0:T(8,128)(2,1)S(1)}, bf16[1024,128]{1,0:T(8,128)(2,1)S(1)}, u32[]{:S(2)}, u32[]{:S(2)}) collective-permute-start(bf16[1024,128]{1,0:T(8,128)(2,1)S(1)} %get-tuple-element.29), channel_id=1, source_target_pairs={{0,128},{128,256},{256,384},{384,512},{512,640},{640,768},{768,896... | collective-permute-start | bytes 786440 | tf_op jit(solution)/shard_map/ppermute | solution.py:289
  60.1 10.7 %collective-permute-start.3 = (bf16[512,512]{1,0:T(8,128)(2,1)S(1)}, bf16[512,512]{1,0:T(8,128)(2,1)S(1)}, u32[]{:S(2)}, u32[]{:S(2)}) collective-permute-start(bf16[512,512]{1,0:T(8,128)(2,1)S(1)} %get-tuple-element.38), channel_id=1, source_target_pairs={{0,1},{1,0},{2,3},{3,2},{4,5},{5,4},{6,7},{7,6},{8,9},{9,8},{10,11... | collective-permute-start | bytes 1572872 | tf_op jit(solution)/shard_map/ppermute | solution.py:340
  63.5 5.3 %copy-start.2 = (bf16[2048,128]{1,0:T(8,128)(2,1)}, bf16[2048,128]{1,0:T(8,128)(2,1)S(1)}, u32[]{:S(2)}) copy-start(bf16[2048,128]{1,0:T(8,128)(2,1)S(1)} %get-tuple-element.41.part_ref) | copy-start | bytes 1572868
  63.5 5.4 %copy-start.4 = (bf16[2048,128]{1,0:T(8,128)(2,1)}, bf16[2048,128]{1,0:T(8,128)(2,1)S(1)}, u32[]{:S(2)}) copy-start(bf16[2048,128]{1,0:T(8,128)(2,1)S(1)} %get-tuple-element.45.part_ref) | copy-start | bytes 1572868
  63.6 16.8 %collective-permute-start.5 = (bf16[2048,128]{1,0:T(8,128)(2,1)S(1)}, bf16[2048,128]{1,0:T(8,128)(2,1)}, u32[]{:S(2)}, u32[]{:S(2)}) collective-permute-start(bf16[2048,128]{1,0:T(8,128)(2,1)S(1)} %behind.3.also_ref), channel_id=1, source_target_pairs={{0,896},{128,0},{256,128},{384,256},{512,384},{640,512},{768,640},... | collective-permute-start | bytes 1572872 | tf_op jit(solution)/shard_map/ppermute | solution.py:305
  68.9 19.4 %collective-permute-start.8 = (bf16[2048,128]{1,0:T(8,128)(2,1)S(1)}, bf16[2048,128]{1,0:T(8,128)(2,1)}, u32[]{:S(2)}, u32[]{:S(2)}) collective-permute-start(bf16[2048,128]{1,0:T(8,128)(2,1)S(1)} %ahead.3.after_ref), channel_id=1, source_target_pairs={{0,128},{128,256},{256,384},{384,512},{512,640},{640,768},{768,896... | collective-permute-start | bytes 1572872 | tf_op jit(solution)/shard_map/ppermute | solution.py:302
  72.2 35.6 %all-to-all-start.1 = ((bf16[64,8,512]{2,1,0:T(8,128)(2,1)}), bf16[64,8,512]{2,1,0:T(8,128)(2,1)S(1)}, u32[]{:S(2)}, u32[]{:S(2)}) async-start(bf16[64,8,512]{2,1,0:T(8,128)(2,1)} %bitcast.7), calls=%async_computation.1 | async-start | bytes 1048576 | tf_op jit(solution)/shard_map/all_to_all | solution.py:327
  80.4 1.0 copy-start.3
  82.6 16.4 %collective-permute-start.6 = (bf16[2048,128]{1,0:T(8,128)(2,1)S(1)}, bf16[2048,128]{1,0:T(8,128)(2,1)S(1)}, u32[]{:S(2)}, u32[]{:S(2)}) collective-permute-start(bf16[2048,128]{1,0:T(8,128)(2,1)S(1)} %behind.4), channel_id=1, source_target_pairs={{0,896},{128,0},{256,128},{384,256},{512,384},{640,512},{768,640},... | collective-permute-start | bytes 1572872 | tf_op jit(solution)/shard_map/ppermute | solution.py:305
  88.3 19.5 %copy-start.5 = (s32[32,1]{0,1:T(1,128)S(1)}, s32[32,1]{0,1:T(1,128)}, u32[]{:S(2)}) copy-start(s32[32,1]{0,1:T(1,128)} %param.6) | copy-start | bytes 388
  89.5 22.1 %copy-start = (f32[128,1024]{1,0:T(8,128)S(1)}, f32[128,1024]{1,0:T(8,128)}, u32[]{:S(2)}) copy-start(f32[128,1024]{1,0:T(8,128)} %tok_ref.3) | copy-start | bytes 1572868
  89.5 22.1 %copy-start.1 = (f32[128,1024]{1,0:T(8,128)S(1)}, f32[128,1024]{1,0:T(8,128)}, u32[]{:S(2)}) copy-start(f32[128,1024]{1,0:T(8,128)} %up_ref.3) | copy-start | bytes 1572868
  89.5 16.2 %collective-permute-start.9 = (bf16[2048,128]{1,0:T(8,128)(2,1)S(1)}, bf16[2048,128]{1,0:T(8,128)(2,1)S(1)}, u32[]{:S(2)}, u32[]{:S(2)}) collective-permute-start(bf16[2048,128]{1,0:T(8,128)(2,1)S(1)} %ahead.4), channel_id=1, source_target_pairs={{0,128},{128,256},{256,384},{384,512},{512,640},{640,768},{768,896... | collective-permute-start | bytes 1572872 | tf_op jit(solution)/shard_map/ppermute | solution.py:302
  99.2 15.4 %collective-permute-start.7 = (bf16[2048,128]{1,0:T(8,128)(2,1)S(1)}, bf16[2048,128]{1,0:T(8,128)(2,1)}, u32[]{:S(2)}, u32[]{:S(2)}) collective-permute-start(bf16[2048,128]{1,0:T(8,128)(2,1)S(1)} %behind.5), channel_id=1, source_target_pairs={{0,896},{128,0},{256,128},{384,256},{512,384},{640,512},{768,640},... | collective-permute-start | bytes 1572872 | tf_op jit(solution)/shard_map/ppermute | solution.py:305
  105.8 15.1 %collective-permute-start.10 = (bf16[2048,128]{1,0:T(8,128)(2,1)S(1)}, bf16[2048,128]{1,0:T(8,128)(2,1)S(1)}, u32[]{:S(2)}, u32[]{:S(2)}) collective-permute-start(bf16[2048,128]{1,0:T(8,128)(2,1)S(1)} %ahead.5), channel_id=1, source_target_pairs={{0,128},{128,256},{256,384},{384,512},{512,640},{640,768},{768,896... | collective-permute-start | bytes 1572872 | tf_op jit(solution)/shard_map/ppermute | solution.py:302
  108.2 3.4 %collective-permute-start.4 = (bf16[256,512]{1,0:T(8,128)(2,1)S(1)}, bf16[256,512]{1,0:T(8,128)(2,1)S(1)}, u32[]{:S(2)}, u32[]{:S(2)}) collective-permute-start(bf16[256,512]{1,0:T(8,128)(2,1)S(1)} %home.1.mine_ref), channel_id=1, source_target_pairs={{0,1},{1,0},{2,3},{3,2},{4,5},{5,4},{6,7},{7,6},{8,9},{9,8},{10,11... | collective-permute-start | bytes 786440 | tf_op jit(solution)/shard_map/ppermute | solution.py:348

commit v6 on v5

--- a/solution.py
+++ b/solution.py
@@ -339,7 +339,7 @@
     )(m, onchip(hidden), onchip(pre_grad), onchip(up_matrix), onchip(down_matrix))
     got = lax.ppermute(send, "mp", swap)
     added = call(functools.partial(add_kernel, block), pltpu.VMEM((rows, half_cols), BF16), 0, "add", 2)(
-        sent[0], sent[1], onchip(keep), onchip(got)
+        sent[1], sent[0], onchip(keep), onchip(got)
     )
     back = exchange(added)
     home = call(functools.partial(home_kernel, block), pltpu.VMEM((2 * tok_rows, half_cols), BF16), 0, "home")(

time: 124 us -> 123 us (level)
  the two profiles are of different devices: /device:TPU:4 before, /device:TPU:52 now
where the time goes in v6:
time: 123 us; the launch traced here: 122 us
  blocking collectives  41.9 us (34%)
  starting transfers between devices  40.3 us (33%)
  waiting for transfers between devices  21.2 us (17%)
  Pallas kernels  16.5 us (13%)
    all_to_all x1, blocking collectives, exchange(): lax.all_to_all(shaped, 'expert', split_axis=0, concat_axis=0, tiled=True)  41.9 us
    ppermute x3, starting transfers between devices, weight_grads(): right = lax.ppermute(sent[-1], 'dp', ahead)  16.5 us
    ppermute x3, waiting for transfers between devices, weight_grads(): right = lax.ppermute(sent[-1], 'dp', ahead)  12.4 us
    pallas_call x12, Pallas kernels, run(): pl.pallas_call(kernel, out_shape=outs, in_specs=[pl.BlockSpec(memory_spac...  10.2 us
    ppermute x3, waiting for transfers between devices, weight_grads(): left = lax.ppermute(sent[-1], 'dp', behind)  7.34 us
    ppermute x3, starting transfers between devices, weight_grads(): left = lax.ppermute(sent[-1], 'dp', behind)  5.89 us
    all_to_all x1, starting transfers between devices, exchange(): lax.all_to_all(shaped, 'expert', split_axis=0, concat_axis=0, tiled=True)  5.21 us
    ppermute x1, starting transfers between devices, weight_grads(): right = lax.ppermute(far_up, 'dp', ahead)  4.82 us
  transfers between devices with their start and end apart: 12, of which 6 were waited for; matrix products, arithmetic and copies ran while one was open for 0% of the time, Pallas kernels for 8%

profile of v6, /device:TPU:52, one launch (start us, length us, event | category | flops | bytes accessed | tf_op | source)
XLA Modules:
  0.0 121.9 jit_solution(14893269757705820548)
XLA Ops:
  0.6 1.6 %slots.1 = bf16[512,512]{1,0:T(8,128)(2,1)S(1)} custom-call(s32[1]{0:T(128)} %bitcast.m_ref, s32[1,32]{1,0:T(1,128)} %bitcast.15, f32[128,1024]{1,0:T(8,128)} %tok_ref.3, f32[128,1024]{1,0:T(8,128)} %up_ref.3), custom_call_target="tpu_custom_call" | custom-call | tf_op jit(solution)/shard_map/slots/pallas_call | solution.py:234
  2.2 41.9 %all_to_all.10 = bf16[64,8,512]{2,1,0:T(8,128)(2,1)S(1)} all-to-all(bf16[64,8,512]{2,1,0:T(8,128)(2,1)S(1)} %bitcast.14), channel_id=1, replica_groups=mesh['dp'=8,'expert'=64,'mp'=2] {'expert'}, dimensions={0} | all-to-all | bytes 1048576 | tf_op jit(solution)/shard_map/all_to_all | solution.py:327
  44.1 1.9 %collective-permute-start = (bf16[512,512]{1,0:T(8,128)(2,1)S(1)}, bf16[512,512]{1,0:T(8,128)(2,1)S(1)}, u32[]{:S(2)}, u32[]{:S(2)}) collective-permute-start(bf16[512,512]{1,0:T(8,128)(2,1)S(1)} %bitcast.11), channel_id=1, source_target_pairs={{0,1},{1,0},{2,3},{3,2},{4,5},{5,4},{6,7},{7,6},{8,9},{9,8},{10,11... | collective-permute-start | bytes 1572872 | tf_op jit(solution)/shard_map/ppermute | solution.py:332
  46.0 2.3 %front.1 = (bf16[512,512]{1,0:T(8,128)(2,1)S(1)}, bf16[1024,1024]{1,0:T(8,128)(2,1)S(1)}, bf16[1024,1024]{1,0:T(8,128)(2,1)S(1)}) custom-call(bf16[512,512]{1,0:T(8,128)(2,1)S(1)} %bitcast.12, bf16[1024,1024]{1,0:T(8,128)(2,1)} %bitcast.17, bf16[1024,1024]{1,0:T(8,128)(2,1)} %bitcast.18), custom_call_target="tpu_custom_call" | custom-call | tf_op jit(solution)/shard_map/front/pallas_call | solution.py:250
  48.3 2.5 %hidden.1 = (bf16[1024,128]{1,0:T(8,128)(2,1)S(1)}, bf16[1024,128]{1,0:T(8,128)(2,1)S(1)}, bf16[256,1024]{1,0:T(8,128)(2,1)S(1)}, bf16[256,1024]{1,0:T(8,128)(2,...) custom-call(s32[1]{0:T(128)} %bitcast.m_ref, s32[1]{0:T(128)} %bitcast.2.group_ref, ...), custom_call_target="tpu_custom_call" | custom-call | tf_op jit(solution)/shard_map/hidden/pallas_call | solution.py:271
  50.8 4.8 %collective-permute-start.2 = (bf16[1024,128]{1,0:T(8,128)(2,1)S(1)}, bf16[1024,128]{1,0:T(8,128)(2,1)S(1)}, u32[]{:S(2)}, u32[]{:S(2)}) collective-permute-start(bf16[1024,128]{1,0:T(8,128)(2,1)S(1)} %get-tuple-element.34), channel_id=1, source_target_pairs={{0,128},{128,256},{256,384},{384,512},{512,640},{640,768},{768,896... | collective-permute-start | bytes 786440 | tf_op jit(solution)/shard_map/ppermute | solution.py:289
  55.6 1.9 %collective-permute-start.1 = (bf16[1024,128]{1,0:T(8,128)(2,1)S(1)}, bf16[1024,128]{1,0:T(8,128)(2,1)S(1)}, u32[]{:S(2)}, u32[]{:S(2)}) collective-permute-start(bf16[1024,128]{1,0:T(8,128)(2,1)S(1)} %get-tuple-element.29), channel_id=1, source_target_pairs={{0,896},{128,0},{256,128},{384,256},{512,384},{640,512},{768,640},... | collective-permute-start | bytes 786440 | tf_op jit(solution)/shard_map/ppermute | solution.py:290
  57.5 1.3 %returns.1 = (f32[512,512]{1,0:T(8,128)S(1)}, bf16[512,512]{1,0:T(8,128)(2,1)S(1)}) custom-call(s32[1]{0:T(128)} %bitcast.m_ref, bf16[256,1024]{1,0:T(8,128)(2,1)S(1)} %get-tuple-element.36.hid_ref, bf16[256,1024]{1,0:T(8,128)(2,1)S(1)} %get-tuple-element.32.pg_ref, bf16[1024,1024]{1,0:T(8,128)(2,1)S(1)} %get-tuple-element.27.up_ref, ...), custom_call_target="tpu_custom_call" | custom-call | tf_op jit(solution)/shard_map/returns/pallas_call | solution.py:215
  58.8 2.1 %collective-permute-start.3 = (bf16[512,512]{1,0:T(8,128)(2,1)S(1)}, bf16[512,512]{1,0:T(8,128)(2,1)S(1)}, u32[]{:S(2)}, u32[]{:S(2)}) collective-permute-start(bf16[512,512]{1,0:T(8,128)(2,1)S(1)} %get-tuple-element.38), channel_id=1, source_target_pairs={{0,1},{1,0},{2,3},{3,2},{4,5},{5,4},{6,7},{7,6},{8,9},{9,8},{10,11... | collective-permute-start | bytes 1572872 | tf_op jit(solution)/shard_map/ppermute | solution.py:340
  60.9 1.2 %shares.1 = (bf16[2048,128]{1,0:T(8,128)(2,1)S(1)}, bf16[2048,128]{1,0:T(8,128)(2,1)S(1)}, bf16[2048,128]{1,0:T(8,128)(2,1)S(1)}, bf16[2048,128]{1,0:T(8,128)(2,...) custom-call(bf16[512,1024]{1,0:T(8,128)(2,1)S(1)} %get-tuple-element.30.turned_r, ...), custom_call_target="tpu_custom_call" | custom-call | tf_op jit(solution)/shard_map/shares/pallas_call | solution.py:215
  62.3 5.2 %collective-permute-start.8 = (bf16[2048,128]{1,0:T(8,128)(2,1)S(1)}, bf16[2048,128]{1,0:T(8,128)(2,1)}, u32[]{:S(2)}, u32[]{:S(2)}) collective-permute-start(bf16[2048,128]{1,0:T(8,128)(2,1)S(1)} %ahead.3.also_ref), channel_id=1, source_target_pairs={{0,128},{128,256},{256,384},{384,512},{512,640},{640,768},{768,896... | collective-permute-start | bytes 1572872 | tf_op jit(solution)/shard_map/ppermute | solution.py:302
  67.6 1.9 %collective-permute-start.5 = (bf16[2048,128]{1,0:T(8,128)(2,1)S(1)}, bf16[2048,128]{1,0:T(8,128)(2,1)}, u32[]{:S(2)}, u32[]{:S(2)}) collective-permute-start(bf16[2048,128]{1,0:T(8,128)(2,1)S(1)} %behind.3.after_ref), channel_id=1, source_target_pairs={{0,896},{128,0},{256,128},{384,256},{512,384},{640,512},{768,640},... | collective-permute-start | bytes 1572872 | tf_op jit(solution)/shard_map/ppermute | solution.py:305
  69.5 1.3 %add.1 = bf16[512,512]{1,0:T(8,128)(2,1)} custom-call(bf16[2048,128]{1,0:T(8,128)(2,1)S(1)} %behind.3.after_ref, bf16[2048,128]{1,0:T(8,128)(2,1)S(1)} %ahead.3.also_ref, f32[512,512]{1,0:T(8,128)S(1)} %get-tuple-element.37.keep_ref, bf16[512,512]{1,0:T(8,128)(2,1)S(1)} %collective-permute-done.3.got_ref), custom_call_target="tpu_custom_call" | custom-call | tf_op jit(solution)/shard_map/add/pallas_call | solution.py:215
  70.8 5.2 %all-to-all-start.1 = ((bf16[64,8,512]{2,1,0:T(8,128)(2,1)}), bf16[64,8,512]{2,1,0:T(8,128)(2,1)S(1)}, u32[]{:S(2)}, u32[]{:S(2)}) async-start(bf16[64,8,512]{2,1,0:T(8,128)(2,1)} %bitcast.7), calls=%async_computation.1 | async-start | bytes 1048576 | tf_op jit(solution)/shard_map/all_to_all | solution.py:327
  76.0 3.0 %collective-permute-done.8.got_ref = bf16[2048,128]{1,0:T(8,128)(2,1)} collective-permute-done((bf16[2048,128]{1,0:T(8,128)(2,1)S(1)}, bf16[2048,128]{1,0:T(8,128)(2,1)}, u32[]{:S(2)}, u32[]{:S(2)}) %collective-permute-start.8) | collective-permute-done | bytes 524320 | tf_op jit(solution)/shard_map/ppermute | solution.py:302
  79.0 1.0 copy-done.3
  80.1 1.2 ahead.4
  81.2 5.7 %collective-permute-start.9 = (bf16[2048,128]{1,0:T(8,128)(2,1)S(1)}, bf16[2048,128]{1,0:T(8,128)(2,1)S(1)}, u32[]{:S(2)}, u32[]{:S(2)}) collective-permute-start(bf16[2048,128]{1,0:T(8,128)(2,1)S(1)} %ahead.4), channel_id=1, source_target_pairs={{0,128},{128,256},{256,384},{384,512},{512,640},{640,768},{768,896... | collective-permute-start | bytes 1572872 | tf_op jit(solution)/shard_map/ppermute | solution.py:302
  87.0 1.2 behind.4
  88.2 2.1 %collective-permute-start.6 = (bf16[2048,128]{1,0:T(8,128)(2,1)S(1)}, bf16[2048,128]{1,0:T(8,128)(2,1)S(1)}, u32[]{:S(2)}, u32[]{:S(2)}) collective-permute-start(bf16[2048,128]{1,0:T(8,128)(2,1)S(1)} %behind.4), channel_id=1, source_target_pairs={{0,896},{128,0},{256,128},{384,256},{512,384},{640,512},{768,640},... | collective-permute-start | bytes 1572872 | tf_op jit(solution)/shard_map/ppermute | solution.py:305
  90.2 7.5 %collective-permute-done.9.got_ref = bf16[2048,128]{1,0:T(8,128)(2,1)S(1)} collective-permute-done((bf16[2048,128]{1,0:T(8,128)(2,1)S(1)}, bf16[2048,128]{1,0:T(8,128)(2,1)S(1)}, u32[]{:S(2)}, u32[]{:S(2)}) %collective-permute-start.9) | collective-permute-done | bytes 524320 | tf_op jit(solution)/shard_map/ppermute | solution.py:302
  97.7 0.1 ahead.5
  97.8 5.6 %collective-permute-start.10 = (bf16[2048,128]{1,0:T(8,128)(2,1)S(1)}, bf16[2048,128]{1,0:T(8,128)(2,1)}, u32[]{:S(2)}, u32[]{:S(2)}) collective-permute-start(bf16[2048,128]{1,0:T(8,128)(2,1)S(1)} %ahead.5), channel_id=1, source_target_pairs={{0,128},{128,256},{256,384},{384,512},{512,640},{640,768},{768,896... | collective-permute-start | bytes 1572872 | tf_op jit(solution)/shard_map/ppermute | solution.py:302
  103.4 0.9 collective-permute-done.6.got_ref
  104.5 1.9 %collective-permute-start.7 = (bf16[2048,128]{1,0:T(8,128)(2,1)S(1)}, bf16[2048,128]{1,0:T(8,128)(2,1)S(1)}, u32[]{:S(2)}, u32[]{:S(2)}) collective-permute-start(bf16[2048,128]{1,0:T(8,128)(2,1)S(1)} %behind.5), channel_id=1, source_target_pairs={{0,896},{128,0},{256,128},{384,256},{512,384},{640,512},{768,640},... | collective-permute-start | bytes 1572872 | tf_op jit(solution)/shard_map/ppermute | solution.py:305
  106.4 0.4 home.1.mine_ref
  106.8 1.9 %collective-permute-start.4 = (bf16[256,512]{1,0:T(8,128)(2,1)S(1)}, bf16[256,512]{1,0:T(8,128)(2,1)S(1)}, u32[]{:S(2)}, u32[]{:S(2)}) collective-permute-start(bf16[256,512]{1,0:T(8,128)(2,1)S(1)} %home.1.mine_ref), channel_id=1, source_target_pairs={{0,1},{1,0},{2,3},{3,2},{4,5},{5,4},{6,7},{7,6},{8,9},{9,8},{10,11... | collective-permute-start | bytes 786440 | tf_op jit(solution)/shard_map/ppermute | solution.py:348
  108.8 1.5 %collective-permute-done.4.other_ref = bf16[256,512]{1,0:T(8,128)(2,1)S(1)} collective-permute-done((bf16[256,512]{1,0:T(8,128)(2,1)S(1)}, bf16[256,512]{1,0:T(8,128)(2,1)S(1)}, u32[]{:S(2)}, u32[]{:S(2)}) %collective-permute-start.4) | collective-permute-done | bytes 262176 | tf_op jit(solution)/shard_map/ppermute | solution.py:348
  110.3 1.0 final.1
  111.3 1.9 %collective-permute-done.10.right_ref = bf16[2048,128]{1,0:T(8,128)(2,1)} collective-permute-done((bf16[2048,128]{1,0:T(8,128)(2,1)S(1)}, bf16[2048,128]{1,0:T(8,128)(2,1)}, u32[]{:S(2)}, u32[]{:S(2)}) %collective-permute-start.10) | collective-permute-done | bytes 524320 | tf_op jit(solution)/shard_map/ppermute | solution.py:302
  113.2 6.4 %collective-permute-done.7.left_ref = bf16[2048,128]{1,0:T(8,128)(2,1)S(1)} collective-permute-done((bf16[2048,128]{1,0:T(8,128)(2,1)S(1)}, bf16[2048,128]{1,0:T(8,128)(2,1)S(1)}, u32[]{:S(2)}, u32[]{:S(2)}) %collective-permute-start.7) | collective-permute-done | bytes 524320 | tf_op jit(solution)/shard_map/ppermute | solution.py:305
  119.6 2.3 %last.1 = (f32[128,1024]{1,0:T(8,128)}, f32[1024,128]{1,0:T(8,128)}) custom-call(f32[128,1024]{1,0:T(8,128)} %get-tuple-element.23.after_ref, bf16[2048,128]{1,0:T(8,128)(2,1)S(1)} %collective-permute-done.7.left_ref, bf16[2048,128]{1,0:T(8,128)(2,1)} %collective-permute-done.10.right_ref, bf16[2048,128]{1,0:T(8,128)(2,1)} %copy-done.4), custom_call_target="tpu_custom_call" | custom-call | tf_op jit(solution)/shard_map/last/pallas_call | solution.py:215
  (20 shorter events, 0.3 us)
Async XLA Ops:
  44.1 4.2 %collective-permute-start = (bf16[512,512]{1,0:T(8,128)(2,1)S(1)}, bf16[512,512]{1,0:T(8,128)(2,1)S(1)}, u32[]{:S(2)}, u32[]{:S(2)}) collective-permute-start(bf16[512,512]{1,0:T(8,128)(2,1)S(1)} %bitcast.11), channel_id=1, source_target_pairs={{0,1},{1,0},{2,3},{3,2},{4,5},{5,4},{6,7},{7,6},{8,9},{9,8},{10,11... | collective-permute-start | bytes 1572872 | tf_op jit(solution)/shard_map/ppermute | solution.py:332
  50.8 11.4 %collective-permute-start.2 = (bf16[1024,128]{1,0:T(8,128)(2,1)S(1)}, bf16[1024,128]{1,0:T(8,128)(2,1)S(1)}, u32[]{:S(2)}, u32[]{:S(2)}) collective-permute-start(bf16[1024,128]{1,0:T(8,128)(2,1)S(1)} %get-tuple-element.34), channel_id=1, source_target_pairs={{0,128},{128,256},{256,384},{384,512},{512,640},{640,768},{768,896... | collective-permute-start | bytes 786440 | tf_op jit(solution)/shard_map/ppermute | solution.py:289
  55.6 11.9 %collective-permute-start.1 = (bf16[1024,128]{1,0:T(8,128)(2,1)S(1)}, bf16[1024,128]{1,0:T(8,128)(2,1)S(1)}, u32[]{:S(2)}, u32[]{:S(2)}) collective-permute-start(bf16[1024,128]{1,0:T(8,128)(2,1)S(1)} %get-tuple-element.29), channel_id=1, source_target_pairs={{0,896},{128,0},{256,128},{384,256},{512,384},{640,512},{768,640},... | collective-permute-start | bytes 786440 | tf_op jit(solution)/shard_map/ppermute | solution.py:290
  58.8 10.7 %collective-permute-start.3 = (bf16[512,512]{1,0:T(8,128)(2,1)S(1)}, bf16[512,512]{1,0:T(8,128)(2,1)S(1)}, u32[]{:S(2)}, u32[]{:S(2)}) collective-permute-start(bf16[512,512]{1,0:T(8,128)(2,1)S(1)} %get-tuple-element.38), channel_id=1, source_target_pairs={{0,1},{1,0},{2,3},{3,2},{4,5},{5,4},{6,7},{7,6},{8,9},{9,8},{10,11... | collective-permute-start | bytes 1572872 | tf_op jit(solution)/shard_map/ppermute | solution.py:340
  62.2 5.3 %copy-start.2 = (bf16[2048,128]{1,0:T(8,128)(2,1)}, bf16[2048,128]{1,0:T(8,128)(2,1)S(1)}, u32[]{:S(2)}) copy-start(bf16[2048,128]{1,0:T(8,128)(2,1)S(1)} %get-tuple-element.43.part_ref) | copy-start | bytes 1572868
  62.2 5.4 %copy-start.4 = (bf16[2048,128]{1,0:T(8,128)(2,1)}, bf16[2048,128]{1,0:T(8,128)(2,1)S(1)}, u32[]{:S(2)}) copy-start(bf16[2048,128]{1,0:T(8,128)(2,1)S(1)} %get-tuple-element.45.part_ref) | copy-start | bytes 1572868
  62.3 16.8 %collective-permute-start.8 = (bf16[2048,128]{1,0:T(8,128)(2,1)S(1)}, bf16[2048,128]{1,0:T(8,128)(2,1)}, u32[]{:S(2)}, u32[]{:S(2)}) collective-permute-start(bf16[2048,128]{1,0:T(8,128)(2,1)S(1)} %ahead.3.also_ref), channel_id=1, source_target_pairs={{0,128},{128,256},{256,384},{384,512},{512,640},{640,768},{768,896... | collective-permute-start | bytes 1572872 | tf_op jit(solution)/shard_map/ppermute | solution.py:302
  67.6 19.4 %collective-permute-start.5 = (bf16[2048,128]{1,0:T(8,128)(2,1)S(1)}, bf16[2048,128]{1,0:T(8,128)(2,1)}, u32[]{:S(2)}, u32[]{:S(2)}) collective-permute-start(bf16[2048,128]{1,0:T(8,128)(2,1)S(1)} %behind.3.after_ref), channel_id=1, source_target_pairs={{0,896},{128,0},{256,128},{384,256},{512,384},{640,512},{768,640},... | collective-permute-start | bytes 1572872 | tf_op jit(solution)/shard_map/ppermute | solution.py:305
  70.8 35.6 %all-to-all-start.1 = ((bf16[64,8,512]{2,1,0:T(8,128)(2,1)}), bf16[64,8,512]{2,1,0:T(8,128)(2,1)S(1)}, u32[]{:S(2)}, u32[]{:S(2)}) async-start(bf16[64,8,512]{2,1,0:T(8,128)(2,1)} %bitcast.7), calls=%async_computation.1 | async-start | bytes 1048576 | tf_op jit(solution)/shard_map/all_to_all | solution.py:327
  79.0 1.0 copy-start.3
  81.2 16.4 %collective-permute-start.9 = (bf16[2048,128]{1,0:T(8,128)(2,1)S(1)}, bf16[2048,128]{1,0:T(8,128)(2,1)S(1)}, u32[]{:S(2)}, u32[]{:S(2)}) collective-permute-start(bf16[2048,128]{1,0:T(8,128)(2,1)S(1)} %ahead.4), channel_id=1, source_target_pairs={{0,128},{128,256},{256,384},{384,512},{512,640},{640,768},{768,896... | collective-permute-start | bytes 1572872 | tf_op jit(solution)/shard_map/ppermute | solution.py:302
  87.0 19.5 %copy-start.5 = (s32[32,1]{0,1:T(1,128)S(1)}, s32[32,1]{0,1:T(1,128)}, u32[]{:S(2)}) copy-start(s32[32,1]{0,1:T(1,128)} %param.6) | copy-start | bytes 388
  88.1 22.1 %copy-start = (f32[128,1024]{1,0:T(8,128)S(1)}, f32[128,1024]{1,0:T(8,128)}, u32[]{:S(2)}) copy-start(f32[128,1024]{1,0:T(8,128)} %tok_ref.3) | copy-start | bytes 1572868
  88.2 22.1 %copy-start.1 = (f32[128,1024]{1,0:T(8,128)S(1)}, f32[128,1024]{1,0:T(8,128)}, u32[]{:S(2)}) copy-start(f32[128,1024]{1,0:T(8,128)} %up_ref.3) | copy-start | bytes 1572868
  88.2 16.2 %collective-permute-start.6 = (bf16[2048,128]{1,0:T(8,128)(2,1)S(1)}, bf16[2048,128]{1,0:T(8,128)(2,1)S(1)}, u32[]{:S(2)}, u32[]{:S(2)}) collective-permute-start(bf16[2048,128]{1,0:T(8,128)(2,1)S(1)} %behind.4), channel_id=1, source_target_pairs={{0,896},{128,0},{256,128},{384,256},{512,384},{640,512},{768,640},... | collective-permute-start | bytes 1572872 | tf_op jit(solution)/shard_map/ppermute | solution.py:305
  97.8 15.4 %collective-permute-start.10 = (bf16[2048,128]{1,0:T(8,128)(2,1)S(1)}, bf16[2048,128]{1,0:T(8,128)(2,1)}, u32[]{:S(2)}, u32[]{:S(2)}) collective-permute-start(bf16[2048,128]{1,0:T(8,128)(2,1)S(1)} %ahead.5), channel_id=1, source_target_pairs={{0,128},{128,256},{256,384},{384,512},{512,640},{640,768},{768,896... | collective-permute-start | bytes 1572872 | tf_op jit(solution)/shard_map/ppermute | solution.py:302
  104.5 15.1 %collective-permute-start.7 = (bf16[2048,128]{1,0:T(8,128)(2,1)S(1)}, bf16[2048,128]{1,0:T(8,128)(2,1)S(1)}, u32[]{:S(2)}, u32[]{:S(2)}) collective-permute-start(bf16[2048,128]{1,0:T(8,128)(2,1)S(1)} %behind.5), channel_id=1, source_target_pairs={{0,896},{128,0},{256,128},{384,256},{512,384},{640,512},{768,640},... | collective-permute-start | bytes 1572872 | tf_op jit(solution)/shard_map/ppermute | solution.py:305
  106.8 3.4 %collective-permute-start.4 = (bf16[256,512]{1,0:T(8,128)(2,1)S(1)}, bf16[256,512]{1,0:T(8,128)(2,1)S(1)}, u32[]{:S(2)}, u32[]{:S(2)}) collective-permute-start(bf16[256,512]{1,0:T(8,128)(2,1)S(1)} %home.1.mine_ref), channel_id=1, source_target_pairs={{0,1},{1,0},{2,3},{3,2},{4,5},{5,4},{6,7},{7,6},{8,9},{9,8},{10,11... | collective-permute-start | bytes 786440 | tf_op jit(solution)/shard_map/ppermute | solution.py:348
